TPU v7x, 32 devices: a whole 2x2x4 slice. The times are simulated.
32 devices in a mesh: seq: 8 (over z, core), tp: 4 (over y, x).
Axes of the slice: x: 2, y: 2, z: 4, core: 2. Of those that a mesh axis runs over, the one named last changes fastest.
Arguments:
- layer_input: bfloat16 [8, 512, 4096], P('seq')
- memory: bfloat16 [8, 512, 4096], P('seq'), may hold values from -6 to 6
- seg_lengths: int32 [8], replicated, may hold values from 257 to 512, as said below
- query_weight: bfloat16 [4096, 4096], P(None, 'tp')
- key_weight: bfloat16 [4096, 4096], P(None, 'tp')
- value_weight: bfloat16 [4096, 4096], P(None, 'tp'), may hold values from -0.09375 to 0.09375
- out_weight: bfloat16 [4096, 4096], P('tp'), may hold values from -0.1875 to 0.1875
Outputs:
- attended: bfloat16 [8, 512, 4096], P('seq', 'tp')
Inputs may be any that keep to these rules, and one draw needn't show every extreme that they name: `seg_lengths`: slots below a segment's count hold real tokens.
All inputs are finite; a program needn't handle non-finite values.
Results may differ from a plain program's by a relative error of at most 0.011.
Values may be sent and summed in bfloat16 or wider, within the bound.
No kernel may reach another device: no remote copies, remote signals or barrier semaphores. Data moves between devices by JAX's collectives and lax.ppermute only.
A program may use at most 128 MiB of HBM per device.

v0:
```python
import math

import jax
import jax.numpy as jnp
from jax import lax
from jax.sharding import PartitionSpec as P

HEAD_DIM = 128


def shifted(x, axis, by):
    devices = lax.axis_size(axis)
    return lax.ppermute(x, axis, [(i, (i + by) % devices) for i in range(devices)])


def project(states, weight):
    return jnp.dot(states, weight, preferred_element_type=jnp.float32).astype(jnp.bfloat16)


def attend_heads(queries, all_keys, all_values, key_ok):
    scores = jnp.einsum(
        "qhd,khd->hqk", queries, all_keys, preferred_element_type=jnp.float32
    ) / math.sqrt(HEAD_DIM)
    row_max = jnp.max(jnp.where(key_ok[None], scores, -1e30), axis=-1, keepdims=True)
    weights = jnp.where(key_ok[None], jnp.exp(scores - row_max), 0.0)
    probabilities = (weights / jnp.sum(weights, axis=-1, keepdims=True)).astype(jnp.bfloat16)
    context = jnp.einsum(
        "hqk,khd->qhd", probabilities, all_values, preferred_element_type=jnp.float32
    )
    return context.astype(jnp.bfloat16)


def body(layer_input, memory, seg_lengths, query_weight, key_weight, value_weight, out_weight):
    seg_count = layer_input.shape[0]
    seg_rows = layer_input.shape[1]
    heads_local = query_weight.shape[1] // HEAD_DIM
    group_index = lax.axis_index("seq")
    seg_total = seg_lengths.shape[0]
    mem_len = lax.dynamic_index_in_dim(
        seg_lengths, jnp.mod(group_index * seg_count - 1, seg_total), 0, keepdims=False
    )
    sent_keys = project(memory[0], key_weight)
    sent_values = project(memory[0], value_weight)
    mem_keys, mem_values = shifted((sent_keys, sent_values), "seq", 1)
    row_ids = jnp.arange(seg_rows, dtype=jnp.int32)[:, None]
    col_ids = jnp.arange(seg_rows, dtype=jnp.int32)[None, :]
    position = group_index * seg_count + 0
    own_len = lax.dynamic_index_in_dim(seg_lengths, position, 0, keepdims=False)
    inputs = layer_input[0]
    queries = project(inputs, query_weight).reshape(seg_rows, heads_local, HEAD_DIM)
    own_keys = project(inputs, key_weight).reshape(seg_rows, heads_local, HEAD_DIM)
    own_values = project(inputs, value_weight).reshape(seg_rows, heads_local, HEAD_DIM)
    mem_ok = jnp.broadcast_to(col_ids < mem_len, (seg_rows, seg_rows))
    own_ok = (col_ids <= row_ids) & (col_ids < own_len)
    key_ok = jnp.concatenate([mem_ok, own_ok], axis=1)
    all_keys = jnp.concatenate(
        [mem_keys.reshape(seg_rows, heads_local, HEAD_DIM), own_keys], axis=0
    )
    all_values = jnp.concatenate(
        [mem_values.reshape(seg_rows, heads_local, HEAD_DIM), own_values], axis=0
    )
    context = attend_heads(queries, all_keys, all_values, key_ok).reshape(
        seg_rows, heads_local * HEAD_DIM
    )
    shared_rows = lax.psum_scatter(
        jnp.dot(context, out_weight, preferred_element_type=jnp.float32),
        "tp",
        scatter_dimension=0,
        tiled=True,
    ).astype(jnp.bfloat16)
    pieces = [shared_rows]
    return jnp.stack(pieces)


def solution(mesh):
    return jax.shard_map(
        body,
        mesh=mesh,
        in_specs=(
            P("seq", None, None),
            P("seq", None, None),
            P(),
            P(None, "tp"),
            P(None, "tp"),
            P(None, "tp"),
            P("tp", None),
        ),
        out_specs=P("seq", "tp", None),
        check_vma=False,
    )
```

profile of v0, /device:TPU:0, one launch (start us, length us, event | category | flops | bytes accessed | tf_op | source)
XLA Modules:
  0.0 204.3 jit_solution(4610114185945078082)
XLA Ops:
  6.5 0.0 reduce-scatter.2.cloned.1.call-start
  6.5 0.0 copy-start.2
  6.5 0.0 copy-start.3
  6.5 10.2 %fusion.29 = bf16[512,1024]{1,0:T(8,128)(2,1)} fusion(bf16[4096,1024]{1,0:T(8,128)(2,1)} %param.11, bf16[1,512,4096]{2,1,0:T(8,128)(2,1)} %param.8), kind=kOutput, calls=%fused_computation.29 | convolution fusion | flops 4295491584 | bytes 13631488 | tf_op jit(solution)/shard_map/dot_general | solution.py:17
  16.8 0.5 collective-permute-start.1
  17.3 0.0 copy-done.2
  17.3 0.0 copy-done.3
  17.3 5.5 %fusion.26 = bf16[512,1024]{1,0:T(8,128)(2,1)} fusion(bf16[4096,1024]{1,0:T(8,128)(2,1)S(1)} %copy-done.2, bf16[1,512,4096]{2,1,0:T(8,128)(2,1)S(1)} %copy-done.3), kind=kOutput, calls=%fused_computation.28 | convolution fusion | flops 4295491584 | bytes 13631488 | tf_op jit(solution)/shard_map/dot_general | solution.py:17
  22.8 2.7 %collective-permute-start = (bf16[512,1024]{1,0:T(8,128)(2,1)}, bf16[512,1024]{1,0:T(8,128)(2,1)S(1)}, u32[]{:S(2)}, u32[]{:S(2)}) collective-permute-start(bf16[512,1024]{1,0:T(8,128)(2,1)} %fusion.26), channel_id=1, source_target_pairs={{0,4},{4,8},{8,12},{12,16},{16,20},{20,24},{24,28},{28,0},{1,5},{5... | collective-permute-start | bytes 3145736 | tf_op jit(solution)/shard_map/ppermute | solution.py:13
  25.4 0.0 copy-start.4
  25.4 10.3 %fusion.44 = bf16[64,8,8,128]{3,2,1,0:T(8,128)(2,1)} fusion(bf16[4096,1024]{1,0:T(8,128)(2,1)} %param.11, bf16[1,512,4096]{2,1,0:T(8,128)(2,1)} %param.7), kind=kOutput, calls=%fused_computation.34 | convolution fusion | flops 4295491584 | bytes 13631488 | tf_op jit(solution)/shard_map/dot_general | solution.py:17
  35.7 0.0 copy-done.4
  35.7 0.0 copy-start.1
  35.7 8.0 %fusion.32 = bf16[512,1024]{1,0:T(8,128)(2,1)} fusion(bf16[4096,1024]{1,0:T(8,128)(2,1)} %param.12, bf16[1,512,4096]{2,1,0:T(8,128)(2,1)S(1)} %copy-done.4), kind=kOutput, calls=%fused_computation.30 | convolution fusion | flops 4295491584 | bytes 13631488 | tf_op jit(solution)/shard_map/dot_general | solution.py:17
  43.7 0.0 copy-done.1
  43.7 0.6 fusion.57
  44.4 0.6 iota_compare_fusion.1
  45.0 0.1 fusion.52
  45.1 0.6 iota_compare_fusion.2
  45.7 1.4 copy.24
  47.1 2.3 %copy.14 = bf16[512,1024]{0,1:T(8,128)(2,1)} copy(bf16[512,1024]{1,0:T(8,128)(2,1)} %fusion.32) | data formatting | bytes 2097152 | tf_op jit(solution)/shard_map/reshape | solution.py:52
  49.4 1.0 pad_add_fusion
  50.4 9.1 %fusion.47 = bf16[64,8,8,128]{3,2,1,0:T(8,128)(2,1)S(1)} fusion(bf16[4096,1024]{1,0:T(8,128)(2,1)} %param.10, bf16[1,512,4096]{2,1,0:T(8,128)(2,1)} %param.7), kind=kOutput, calls=%fused_computation.35 | convolution fusion | flops 4295491584 | bytes 13631488 | tf_op jit(solution)/shard_map/dot_general | solution.py:17
  59.6 0.0 collective-permute-done.1
  59.6 0.2 copy_bitcast_fusion.1
  59.8 8.1 %fusion.22 = f32[8,512,1024]{2,1,0:T(8,128)} fusion(bf16[512,8,128]{2,0,1:T(8,128)(2,1)S(1)} %bitcast.57, bf16[512,8,128]{2,0,1:T(8,128)(2,1)S(1)} %copy_bitcast_fusion.1, bf16[64,8,8,128]{3,2,1,0:T(8,128)(2,1)S(1)} %fusion.47), kind=kOutput, calls=%fused_computation.23 | convolution fusion | flops 1077936128 | bytes 19922944 | tf_op jit(solution)/shard_map/qhd,khd->hqk/dot_general | solution.py:21
  67.8 0.0 copy-start
  67.8 22.1 %fusion.58 = (f32[8,512]{1,0:T(8,128)S(1)}, f32[8,512,1024]{2,1,0:T(8,128)}) fusion(f32[8,512,1024]{2,1,0:T(8,128)} %fusion.22, pred[512,1024]{1,0:T(8,128)(4,1)} %pad_add_fusion), kind=kOutput, calls=%fused_computation.50 | output fusion | flops 25166848 | bytes 34095104 | tf_op jit(solution)/shard_map/sub | solution.py:25
  90.0 0.0 collective-permute-done
  90.0 0.5 copy.13
  90.5 0.0 copy-done
  90.5 7.4 %fusion.41 = bf16[8,128,512]{2,1,0:T(8,128)(2,1)S(1)} fusion(f32[8,512,1024]{2,1,0:T(8,128)} %get-tuple-element.8, f32[8,512]{1,0:T(8,128)S(1)} %get-tuple-element.7, bf16[512,8,128]{0,2,1:T(8,128)(2,1)S(1)} %bitcast.59, bf16[512,8,128]{0,2,1:T(8,128)(2,1)S(1)} %bitcast.60), kind=kOutput, calls=%fused_computation.33 | convolution fusion | flops 1086849024 | bytes 19939328 | tf_op jit(solution)/shard_map/hqk,khd->qhd/dot_general | solution.py:27
  97.9 10.2 %fusion.59 = f32[512,4096]{1,0:T(8,128)} fusion(bf16[512,1024]{0,1:T(8,128)(2,1)S(1)} %bitcast.58, bf16[1024,4096]{1,0:T(8,128)(2,1)} %param.13), kind=kOutput, calls=%fused_computation.51 | convolution fusion | flops 4294967296 | bytes 17825792 | tf_op jit(solution)/shard_map/dot_general | solution.py:66
  108.1 0.0 reduce-scatter.2.cloned.1.call-update
  108.1 86.7 %reduce-scatter.2.cloned.1.call-done = f32[128,4096]{1,0:T(8,128)} async-done(((f32[512,4096]{1,0:T(8,128)}), f32[128,4096]{1,0:T(8,128)}) %reduce-scatter.2.cloned.1.call-update) | async-done | bytes 2097168 | tf_op jit(solution)/shard_map/reduce_scatter | solution.py:65
  194.8 2.7 %convert_bitcast_fusion = bf16[1,128,4096]{2,1,0:T(8,128)(2,1)} fusion(f32[128,4096]{1,0:T(8,128)} %reduce-scatter.2.cloned.1.call-done), kind=kLoop, calls=%fused_computation.40 | loop fusion | flops 524288 | bytes 3145728 | tf_op jit(solution)/shard_map/stack | solution.py:72
  (1 shorter events, 0.0 us)
Async XLA Ops:
  6.5 188.3 %reduce-scatter.2.cloned.1.call-start = ((), (), s32[]{:S(2)}) async-start(), calls=%async_computation.1 | async-start | bytes 10485760 | tf_op jit(solution)/shard_map/reduce_scatter | solution.py:65
  6.5 10.7 %copy-start.2 = (bf16[4096,1024]{1,0:T(8,128)(2,1)S(1)}, bf16[4096,1024]{1,0:T(8,128)(2,1)}, u32[]{:S(2)}) copy-start(bf16[4096,1024]{1,0:T(8,128)(2,1)} %param.12) | copy-start | bytes 25165828
  6.5 10.7 %copy-start.3 = (bf16[1,512,4096]{2,1,0:T(8,128)(2,1)S(1)}, bf16[1,512,4096]{2,1,0:T(8,128)(2,1)}, u32[]{:S(2)}) copy-start(bf16[1,512,4096]{2,1,0:T(8,128)(2,1)} %param.8) | copy-start | bytes 12582916
  16.8 42.8 %collective-permute-start.1 = (bf16[512,1024]{1,0:T(8,128)(2,1)}, bf16[512,1024]{1,0:T(8,128)(2,1)S(1)}, u32[]{:S(2)}, u32[]{:S(2)}) collective-permute-start(bf16[512,1024]{1,0:T(8,128)(2,1)} %fusion.29), channel_id=1, source_target_pairs={{0,4},{4,8},{8,12},{12,16},{16,20},{20,24},{24,28},{28,0},{1,5},{5... | collective-permute-start | bytes 3145736 | tf_op jit(solution)/shard_map/ppermute | solution.py:13
  22.8 67.2 %collective-permute-start = (bf16[512,1024]{1,0:T(8,128)(2,1)}, bf16[512,1024]{1,0:T(8,128)(2,1)S(1)}, u32[]{:S(2)}, u32[]{:S(2)}) collective-permute-start(bf16[512,1024]{1,0:T(8,128)(2,1)} %fusion.26), channel_id=1, source_target_pairs={{0,4},{4,8},{8,12},{12,16},{16,20},{20,24},{24,28},{28,0},{1,5},{5... | collective-permute-start | bytes 3145736 | tf_op jit(solution)/shard_map/ppermute | solution.py:13
  25.4 10.3 %copy-start.4 = (bf16[1,512,4096]{2,1,0:T(8,128)(2,1)S(1)}, bf16[1,512,4096]{2,1,0:T(8,128)(2,1)}, u32[]{:S(2)}) copy-start(bf16[1,512,4096]{2,1,0:T(8,128)(2,1)} %param.7) | copy-start | bytes 12582916
  35.7 8.0 %copy-start.1 = (s32[8]{0:T(128)S(1)}, s32[8]{0:T(128)}, u32[]{:S(2)}) copy-start(s32[8]{0:T(128)} %param.9) | copy-start | bytes 100
  67.8 22.7 %copy-start = (bf16[512,1024]{0,1:T(8,128)(2,1)S(1)}, bf16[512,1024]{0,1:T(8,128)(2,1)}, u32[]{:S(2)}) copy-start(bf16[512,1024]{0,1:T(8,128)(2,1)} %copy.14) | copy-start | bytes 3145732
Sparse Core Ops, SparseCore 0:
  108.2 86.5 reduce-scatter.1
where the time goes:
time: 205 us; the launch traced here: 204 us
  waiting for transfers between devices  86.7 us (42%)
  matrix products  68.8 us (34%)
  other arithmetic  27.1 us (13%)
  between operations  13.5 us (7%)
  local copies, waits for them, and re-layouts  5.08 us (2%)
  starting transfers between devices  3.17 us (2%)
    reduce_scatter x1, waiting for transfers between devices, body(): lax.psum_scatter(jnp.dot(context, out_weight, preferred_element_type=jnp....  86.7 us
    dot_general x5, matrix products, project(): jnp.dot(states, weight, preferred_element_type=jnp.float32)  43.1 us
    sub x1, other arithmetic, attend_heads(): weights = jnp.where(key_ok[None], jnp.exp(scores - row_max), 0.0)  22.1 us
    dot_general x1, matrix products, body(): jnp.dot(context, out_weight, preferred_element_type=jnp.float32)  10.2 us
    dot_general x1, matrix products, attend_heads(): jnp.einsum('qhd,khd->hqk', queries, all_keys, preferred_element_type=jnp....  8.07 us
    dot_general x1, matrix products, attend_heads(): jnp.einsum('hqk,khd->qhd', probabilities, all_values, preferred_element_t...  7.4 us
  transfers between devices with their start and end apart: 3, of which 1 were waited for; matrix products, arithmetic and copies ran while one was open for 34% of the time, Pallas kernels for 0%

commit v1 on v0

v1 whole, which is shorter than its diff:
```python
import functools
import math

import jax
import jax.numpy as jnp
from jax import lax
from jax.experimental import pallas as pl
from jax.experimental.pallas import tpu as pltpu
from jax.sharding import PartitionSpec as P

HEAD_DIM = 128
TILE = 256
PARTS = 4
VMEM = pltpu.VMEM
BF16 = jnp.bfloat16
F32 = jnp.float32


def dot(a, b):
    return jnp.dot(a, b, preferred_element_type=F32)


def tile_of(index, size):
    return pl.ds(pl.multiple_of(index * size, size), size)


def params(limit_mib):
    return pltpu.CompilerParams(vmem_limit_bytes=limit_mib << 20)


def cost(rows, depth, cols, extra=0):
    return pl.CostEstimate(
        flops=2 * rows * depth * cols,
        bytes_accessed=2 * (rows * depth + depth * cols + rows * cols) + extra,
        transcendentals=0,
    )


def streamed_kernel(x_hbm, w_hbm, out, x, w, x_sem, w_sem, tile_sem):
    depth, cols = w_hbm.shape
    part = depth // PARTS
    tiles = cols // TILE
    first = []
    for k in range(PARTS):
        rows = pl.ds(k * part, part)
        cx = pltpu.make_async_copy(x_hbm.at[:, rows], x.at[:, rows], x_sem.at[k])
        cw = pltpu.make_async_copy(
            w_hbm.at[rows, pl.ds(0, TILE)], w.at[0, rows, :], w_sem.at[k]
        )
        cx.start()
        cw.start()
        first.append((cx, cw))

    def fetch(j):
        return pltpu.make_async_copy(
            w_hbm.at[:, tile_of(j, TILE)], w.at[lax.rem(j, 2)], tile_sem.at[lax.rem(j, 2)]
        )

    if tiles > 1:
        fetch(1).start()
    total = None
    for k in range(PARTS):
        first[k][0].wait()
        first[k][1].wait()
        rows = pl.ds(k * part, part)
        term = dot(x[:, rows], w[0, rows, :])
        total = term if total is None else total + term
    out[:, pl.ds(0, TILE)] = total.astype(BF16)
    if tiles > 2:
        fetch(2).start()

    def step(j, carry):
        fetch(j).wait()
        out[:, tile_of(j, TILE)] = dot(x[...], w[lax.rem(j, 2)]).astype(BF16)

        @pl.when(j + 2 < tiles)
        def _():
            fetch(j + 2).start()

        return carry

    lax.fori_loop(1, tiles, step, 0)


def streamed(x, w):
    rows, depth = x.shape
    cols = w.shape[1]
    return pl.pallas_call(
        streamed_kernel,
        out_shape=jax.ShapeDtypeStruct((rows, cols), BF16),
        in_specs=[pl.BlockSpec(memory_space=pltpu.HBM)] * 2,
        out_specs=pl.BlockSpec(memory_space=VMEM),
        scratch_shapes=[
            VMEM((rows, depth), BF16),
            VMEM((2, depth, TILE), BF16),
            pltpu.SemaphoreType.DMA((PARTS,)),
            pltpu.SemaphoreType.DMA((PARTS,)),
            pltpu.SemaphoreType.DMA((2,)),
        ],
        compiler_params=params(12),
        cost_estimate=cost(rows, depth, cols),
    )(pltpu.with_memory_space_constraint(x, pltpu.HBM), pltpu.with_memory_space_constraint(w, pltpu.HBM))


def resident_kernel(count, x, *refs):
    cols = refs[0].shape[1]
    for w, out in zip(refs[:count], refs[count:]):

        def step(j, carry, w=w, out=out):
            out[:, tile_of(j, TILE)] = dot(x[...], w[:, tile_of(j, TILE)]).astype(BF16)
            return carry

        lax.fori_loop(0, cols // TILE, step, 0)


def resident(x, *ws):
    rows, depth = x.shape
    cols = ws[0].shape[1]
    count = len(ws)
    out = pl.pallas_call(
        functools.partial(resident_kernel, count),
        out_shape=[jax.ShapeDtypeStruct((rows, cols), BF16)] * count,
        in_specs=[pl.BlockSpec(memory_space=VMEM)] * (1 + count),
        out_specs=[pl.BlockSpec(memory_space=VMEM)] * count,
        compiler_params=params(4),
        cost_estimate=cost(rows, depth, cols * count),
    )(x, *ws)
    return out


def attend_kernel(blocks_of, split, lens, x, wq, km, vm, ko, vo, wo, *refs):
    blocks = blocks_of()
    outs = refs[: len(split)]
    q, bias, ctx = refs[len(split) :]
    rows = q.shape[0] // len(blocks)
    keys = ko.shape[0]
    width = wq.shape[1]
    group = lax.axis_index("seq")
    total = lens.shape[0]
    own_len = lens[group]
    mem_len = lens[lax.rem(group + total - 1, total)]
    tile = min(TILE, width)
    for n, b in enumerate(blocks):
        here = pl.ds(n * rows, rows)
        start = pl.multiple_of(b * rows, rows)
        row = lax.broadcasted_iota(jnp.int32, (rows, keys), 0) + start
        col = lax.broadcasted_iota(jnp.int32, (rows, keys), 1)
        bias[here, pl.ds(0, keys)] = jnp.where(col < mem_len, 0.0, -1e30)
        bias[here, pl.ds(keys, keys)] = jnp.where((col <= row) & (col < own_len), 0.0, -1e30)

    def project(j, carry):
        for n, b in enumerate(blocks):
            q[pl.ds(n * rows, rows), tile_of(j, tile)] = dot(
                x[tile_of(b, rows), :], wq[:, tile_of(j, tile)]
            ).astype(BF16)
        return carry

    lax.fori_loop(0, width // tile, project, 0)
    scale = math.log2(math.e) / math.sqrt(HEAD_DIM)

    def head(h, carry):
        lanes = tile_of(h, HEAD_DIM)
        query = q[:, lanes]
        nt = (((1,), (1,)), ((), ()))
        sm = lax.dot_general(query, km[:, lanes], nt, preferred_element_type=F32)
        so = lax.dot_general(query, ko[:, lanes], nt, preferred_element_type=F32)
        sm = sm + bias[:, pl.ds(0, keys)]
        so = so + bias[:, pl.ds(keys, keys)]
        top = jnp.maximum(
            jnp.max(sm, axis=-1, keepdims=True), jnp.max(so, axis=-1, keepdims=True)
        )
        pm = jnp.exp2((sm - top) * scale)
        po = jnp.exp2((so - top) * scale)
        norm = jnp.sum(pm, axis=-1, keepdims=True) + jnp.sum(po, axis=-1, keepdims=True)
        mixed = dot(pm.astype(BF16), vm[:, lanes]) + dot(po.astype(BF16), vo[:, lanes])
        ctx[:, lanes] = (mixed / norm).astype(BF16)
        return carry

    lax.fori_loop(0, width // HEAD_DIM, head, 0)
    for out, (block, first, cols) in zip(outs, split):
        here = pl.ds(block * rows, rows)

        def step(j, carry, out=out, here=here, first=first):
            out[:, tile_of(j, TILE)] = dot(
                ctx[here, :], wo[:, tile_of(j + first // TILE, TILE)]
            ).astype(out.dtype)
            return carry

        lax.fori_loop(0, cols // TILE, step, 0)


def attend(blocks_of, count, split, kinds, rows, lens, x, wq, km, vm, ko, vo, wo):
    keys = ko.shape[0]
    depth, width = wq.shape
    flops = 2 * count * rows * (2 * depth * width + 2 * width * 2 * keys)
    return pl.pallas_call(
        functools.partial(attend_kernel, blocks_of, split),
        out_shape=[
            jax.ShapeDtypeStruct((rows, cols), kind) for (_, _, cols), kind in zip(split, kinds)
        ],
        in_specs=[pl.BlockSpec(memory_space=pltpu.SMEM)] + [pl.BlockSpec(memory_space=VMEM)] * 7,
        out_specs=[pl.BlockSpec(memory_space=VMEM)] * len(split),
        scratch_shapes=[
            VMEM((count * rows, width), BF16),
            VMEM((count * rows, 2 * keys), F32),
            VMEM((count * rows, width), BF16),
        ],
        compiler_params=params(12),
        cost_estimate=pl.CostEstimate(
            flops=flops, bytes_accessed=4 * depth * width, transcendentals=0
        ),
    )(lens, x, wq, km, vm, ko, vo, wo)


def shifted(x, axis, by):
    devices = lax.axis_size(axis)
    return lax.ppermute(x, axis, [(i, (i + by) % devices) for i in range(devices)])


def swapped(x, bit):
    return lax.ppermute(x, "tp", [(i, i ^ bit) for i in range(lax.axis_size("tp"))])


def add_kernel(a, b, out):
    out[...] = (a[...] + b[...].astype(F32)).astype(BF16)


def add(a, b):
    return pl.pallas_call(
        add_kernel,
        out_shape=jax.ShapeDtypeStruct(a.shape, BF16),
        in_specs=[pl.BlockSpec(memory_space=VMEM)] * 2,
        out_specs=pl.BlockSpec(memory_space=VMEM),
        compiler_params=params(4),
        cost_estimate=pl.CostEstimate(flops=a.size, bytes_accessed=8 * a.size, transcendentals=0),
    )(a, b)


def final_kernel(own, xa, xb, ya, yb, out):
    half = xa.shape[1]
    left, right = pl.ds(0, half), pl.ds(half, half)
    out[0, :, left] = (own[:, left] + xa[...].astype(F32) + ya[...].astype(F32)).astype(BF16)
    out[0, :, right] = (own[:, right] + xb[...].astype(F32) + yb[...].astype(F32)).astype(BF16)


def final(own, *parts):
    return pl.pallas_call(
        final_kernel,
        out_shape=jax.ShapeDtypeStruct((1, *own.shape), BF16),
        in_specs=[pl.BlockSpec(memory_space=VMEM)] * 5,
        out_specs=pl.BlockSpec(memory_space=VMEM),
        compiler_params=params(4),
        cost_estimate=pl.CostEstimate(
            flops=3 * own.size, bytes_accessed=14 * own.size, transcendentals=0
        ),
    )(own, *parts)


def body(layer_input, memory, lens, wq, wk, wv, wo):
    seg_rows = layer_input.shape[1]
    shares = lax.axis_size("tp")
    x, m = layer_input[0], memory[0]
    rows = seg_rows // shares
    half = wo.shape[1] // 2
    sent_keys = streamed(m, wk)
    mem_keys = shifted(sent_keys, "seq", 1)
    (sent_values,) = resident(m, wv)
    mem_values = shifted(sent_values, "seq", 1)
    own_keys, own_values = resident(x, wk, wv)
    operands = (lens, x, wq, mem_keys, mem_values, own_keys, own_values, wo)

    if shares != 4:

        def every():
            return [jnp.int32(b) for b in range(shares)]

        terms = attend(
            every,
            shares,
            tuple((b, 0, 2 * half) for b in range(shares)),
            (F32,) * shares,
            rows,
            *operands,
        )
        summed = lax.psum_scatter(
            jnp.concatenate(terms), "tp", scatter_dimension=0, tiled=True
        )
        return summed.astype(BF16)[None]

    def far():
        return [lax.axis_index("tp") ^ 3]

    def near():
        return [lax.axis_index("tp") ^ 1, lax.axis_index("tp") ^ 2]

    def mine():
        return [lax.axis_index("tp")]

    far_a, far_b = attend(far, 1, ((0, 0, half), (0, half, half)), (BF16, BF16), rows, *operands)
    got_a, got_b = swapped(far_a, 1), swapped(far_b, 2)
    xa, xb, ya, yb = attend(
        near,
        2,
        ((0, 0, half), (0, half, half), (1, 0, half), (1, half, half)),
        (BF16, F32, F32, BF16),
        rows,
        *operands,
    )
    from_xa, from_yb = swapped(xa, 1), swapped(yb, 2)
    from_xb, from_ya = swapped(add(xb, got_b), 1), swapped(add(ya, got_a), 2)
    (own,) = attend(mine, 1, ((0, 0, 2 * half),), (F32,), rows, *operands)
    return final(own, from_xa, from_xb, from_ya, from_yb)


def solution(mesh):
    return jax.shard_map(
        body,
        mesh=mesh,
        in_specs=(
            P("seq", None, None),
            P("seq", None, None),
            P(),
            P(None, "tp"),
            P(None, "tp"),
            P(None, "tp"),
            P("tp", None),
        ),
        out_specs=P("seq", "tp", None),
        check_vma=False,
    )
```

time: 205 us -> 93.2 us (0.45)
  waiting for transfers between devices: 86.7 us -> 16.2 us
  matrix products: 68.8 us -> 0 us
  Pallas kernels: 0 us -> 65.5 us
  other arithmetic: 27.1 us -> 0.01 us
  between operations: 13.5 us -> 0.18 us
  starting transfers between devices: 3.17 us -> 11.1 us
  local copies, waits for them, and re-layouts: 5.08 us -> 0.05 us
    reduce_scatter x1 -> x0, waiting for transfers between devices: 86.7 us -> none  [body(): lax.psum_scatter(jnp.dot(context, out_weight, preferred_element_type=jnp....]
    dot_general x8 -> x0, matrix products: 68.8 us -> none  [the longest x5 43.1 us: project(): jnp.dot(states, weight, preferred_element_type=jnp.float32)]
    pallas_call x0 -> x9, Pallas kernels: none -> 65.5 us  [the longest x3 39.2 us: attend(): pl.pallas_call(functools.partial(attend_kernel, blocks_of, split), out_sh...]
    sub x1 -> x0, other arithmetic: 22.1 us -> none  [attend_heads(): weights = jnp.where(key_ok[None], jnp.exp(scores - row_max), 0.0)]
    ppermute x2, waiting for transfers between devices: 0.01 us -> 9.42 us  [shifted(): lax.ppermute(x, axis, [(i, (i + by) % devices) for i in range(devices)])]
    ppermute x0 -> x6, starting transfers between devices: none -> 7.82 us  [swapped(): lax.ppermute(x, 'tp', [(i, i ^ bit) for i in range(lax.axis_size('tp'))])]
    ppermute x0 -> x6, waiting for transfers between devices: none -> 6.76 us  [swapped(): lax.ppermute(x, 'tp', [(i, i ^ bit) for i in range(lax.axis_size('tp'))])]
    reshape x4 -> x0, local copies, waits for them, and re-layouts: 4.42 us -> none  [the longest x1 2.28 us: body(): project(inputs, value_weight).reshape(seg_rows, heads_local, HEAD_DIM)]
  transfers between devices with their start and end apart: 3 -> 8, of which waited for: 1 -> 2; matrix products, arithmetic and copies ran while one was open for 34% -> 0% of each run, Pallas kernels for 0% -> 47%
where the time goes in v1:
time: 93.2 us; the launch traced here: 93 us
  Pallas kernels  65.5 us (70%)
  waiting for transfers between devices  16.2 us (17%)
  starting transfers between devices  11.1 us (12%)
    pallas_call x3, Pallas kernels, attend(): pl.pallas_call(functools.partial(attend_kernel, blocks_of, split), out_sh...  39.2 us
    pallas_call x2, Pallas kernels, resident(): pl.pallas_call(functools.partial(resident_kernel, count), out_shape=[jax....  15.5 us
    ppermute x2, waiting for transfers between devices, shifted(): lax.ppermute(x, axis, [(i, (i + by) % devices) for i in range(devices)])  9.42 us
    pallas_call x1, Pallas kernels, streamed(): pl.pallas_call(streamed_kernel, out_shape=jax.ShapeDtypeStruct((rows, col...  9.29 us
    ppermute x6, starting transfers between devices, swapped(): lax.ppermute(x, 'tp', [(i, i ^ bit) for i in range(lax.axis_size('tp'))])  7.82 us
    ppermute x6, waiting for transfers between devices, swapped(): lax.ppermute(x, 'tp', [(i, i ^ bit) for i in range(lax.axis_size('tp'))])  6.76 us
    ppermute x2, starting transfers between devices, shifted(): lax.ppermute(x, axis, [(i, (i + by) % devices) for i in range(devices)])  3.27 us
  transfers between devices with their start and end apart: 8, of which 2 were waited for; matrix products, arithmetic and copies ran while one was open for 0% of the time, Pallas kernels for 47%

profile of v1, /device:TPU:0, one launch (start us, length us, event | category | flops | bytes accessed | tf_op | source)
XLA Modules:
  0.0 93.0 jit_solution(16444213539974821656)
XLA Ops:
  0.0 0.0 copy-start.3
  0.0 0.0 copy-start.2
  0.0 0.0 slice-start.4
  0.0 9.3 %shard_map.73 = bf16[512,1024]{1,0:T(8,128)(2,1)S(1)} custom-call(bf16[512,4096]{1,0:T(8,128)(2,1)} %bitcast.12, bf16[4096,1024]{1,0:T(8,128)(2,1)} %refs_0_.3), custom_call_target="tpu_custom_call" | custom-call | flops 4294967296 | bytes 13631488 | tf_op jit(solution)/shard_map/pallas_call | solution.py:88
  9.3 0.0 copy-start
  9.3 0.0 slice-start.5
  9.3 0.6 collective-permute-start
  9.9 0.0 copy-done.3
  9.9 0.0 copy-done.2
  9.9 0.0 slice-start
  9.9 0.0 slice-start.2
  9.9 5.2 %shard_map.74 = bf16[512,1024]{1,0:T(8,128)(2,1)S(1)} custom-call(bf16[512,4096]{1,0:T(8,128)(2,1)S(1)} %bitcast.13, bf16[4096,1024]{1,0:T(8,128)(2,1)S(1)} %copy-done.2), custom_call_target="tpu_custom_call" | custom-call | flops 4294967296 | bytes 13631488 | tf_op jit(solution)/shard_map/pallas_call | solution.py:120
  15.1 2.7 %collective-permute-start.1 = (bf16[512,1024]{1,0:T(8,128)(2,1)S(1)}, bf16[512,1024]{1,0:T(8,128)(2,1)S(1)}, u32[]{:S(2)}, u32[]{:S(2)}) collective-permute-start(bf16[512,1024]{1,0:T(8,128)(2,1)S(1)} %shard_map.74), channel_id=1, source_target_pairs={{0,4},{4,8},{8,12},{12,16},{16,20},{20,24},{24,28},{28,0},{1,5},{5... | collective-permute-start | bytes 3145736 | tf_op jit(solution)/shard_map/ppermute | solution.py:217
  17.8 0.0 slice-done.4
  17.8 0.0 copy-done
  17.8 0.0 slice-done.5
  17.8 0.0 slice-start.1
  17.8 0.0 slice-start.3
  17.8 0.0 copy-start.1
  17.9 10.3 %shard_map.75 = (bf16[512,1024]{1,0:T(8,128)(2,1)S(1)}, bf16[512,1024]{1,0:T(8,128)(2,1)S(1)}) custom-call(bf16[512,4096]{1,0:T(8,128)(2,1)S(1)} %bitcast.6, bf16[4096,1024]{1,0:T(8,128)(2,1)S(1)} %bitcast.11, bf16[4096,1024]{1,0:T(8,128)(2,1)S(1)} %copy-done.2), custom_call_target="tpu_custom_call" | custom-call | flops 8589934592 | bytes 23068672 | tf_op jit(solution)/shard_map/pallas_call | solution.py:120
  28.2 0.0 collective-permute-done.km
  28.2 9.4 %collective-permute-done.1.vm = bf16[512,1024]{1,0:T(8,128)(2,1)S(1)} collective-permute-done((bf16[512,1024]{1,0:T(8,128)(2,1)S(1)}, bf16[512,1024]{1,0:T(8,128)(2,1)S(1)}, u32[]{:S(2)}, u32[]{:S(2)}) %collective-permute-start.1) | collective-permute-done | bytes 1048608 | tf_op jit(solution)/shard_map/ppermute | solution.py:217
  37.6 0.0 slice-done
  37.6 0.0 slice-done.2
  37.6 0.0 slice-done.1
  37.6 0.0 slice-done.3
  37.6 0.0 copy-done.1
  37.7 11.0 %shard_map.78 = (bf16[128,2048]{1,0:T(8,128)(2,1)S(1)}, bf16[128,2048]{1,0:T(8,128)(2,1)S(1)}) custom-call(s32[8]{0:T(128)S(1)} %copy-done.1, bf16[512,4096]{1,0:T(8,128)(2,1)S(1)} %bitcast.7, bf16[4096,1024]{1,0:T(8,128)(2,1)S(1)} %bitcast.3, bf16[512,1024]{1,0:T(8,128)(2,1)S(1)} %collective-permute-done.km, ...), custom_call_target="tpu_custom_call" | custom-call | flops 2684354560 | bytes 16777216 | tf_op jit(solution)/shard_map/pallas_call | solution.py:196
  48.7 2.1 %collective-permute-start.5 = (bf16[128,2048]{1,0:T(8,128)(2,1)S(1)}, bf16[128,2048]{1,0:T(8,128)(2,1)S(1)}, u32[]{:S(2)}, u32[]{:S(2)}) collective-permute-start(bf16[128,2048]{1,0:T(8,128)(2,1)S(1)} %get-tuple-element.19), channel_id=1, source_target_pairs={{0,1},{1,0},{2,3},{3,2},{4,5},{5,4},{6,7},{7,6},{8,9},{9,8},{10,11... | collective-permute-start | bytes 1572872 | tf_op jit(solution)/shard_map/ppermute | solution.py:221
  50.7 1.5 %collective-permute-start.3 = (bf16[128,2048]{1,0:T(8,128)(2,1)S(1)}, bf16[128,2048]{1,0:T(8,128)(2,1)S(1)}, u32[]{:S(2)}, u32[]{:S(2)}) collective-permute-start(bf16[128,2048]{1,0:T(8,128)(2,1)S(1)} %get-tuple-element.17), channel_id=1, source_target_pairs={{0,2},{1,3},{2,0},{3,1},{4,6},{5,7},{6,4},{7,5},{8,10},{9,11},{10,... | collective-permute-start | bytes 1572872 | tf_op jit(solution)/shard_map/ppermute | solution.py:221
  52.2 17.2 %shard_map.77 = (bf16[128,2048]{1,0:T(8,128)(2,1)S(1)}, f32[128,2048]{1,0:T(8,128)S(1)}, f32[128,2048]{1,0:T(8,128)S(1)}, bf16[128,2048]{1,0:T(8,128)(2,1)S(1)}) custom-call(s32[8]{0:T(128)S(1)} %copy-done.1, bf16[512,4096]{1,0:T(8,128)(2,1)S(1)} %bitcast.8, bf16[4096,1024]{1,0:T(8,128)(2,1)S(1)} %bitcast.3, bf16[512,1024]{1,0:T(8,128)(2,1)S(1)} %collective-permute-done.km, ...), custom_call_target="tpu_custom_call" | custom-call | flops 5368709120 | bytes 16777216 | tf_op jit(solution)/shard_map/pallas_call | solution.py:196
  69.5 0.6 collective-permute-start.2
  70.1 0.0 collective-permute-start.7
  70.1 0.0 collective-permute-done.5.b
  70.1 0.1 shard_map.80
  70.3 2.0 %collective-permute-start.6 = (bf16[128,2048]{1,0:T(8,128)(2,1)S(1)}, bf16[128,2048]{1,0:T(8,128)(2,1)S(1)}, u32[]{:S(2)}, u32[]{:S(2)}) collective-permute-start(bf16[128,2048]{1,0:T(8,128)(2,1)S(1)} %shard_map.80), channel_id=1, source_target_pairs={{0,2},{1,3},{2,0},{3,1},{4,6},{5,7},{6,4},{7,5},{8,10},{9,11},{10,... | collective-permute-start | bytes 1572872 | tf_op jit(solution)/shard_map/ppermute | solution.py:221
  72.3 0.0 collective-permute-done.3.b
  72.3 0.1 shard_map.79
  72.4 1.6 %collective-permute-start.4 = (bf16[128,2048]{1,0:T(8,128)(2,1)S(1)}, bf16[128,2048]{1,0:T(8,128)(2,1)S(1)}, u32[]{:S(2)}, u32[]{:S(2)}) collective-permute-start(bf16[128,2048]{1,0:T(8,128)(2,1)S(1)} %shard_map.79), channel_id=1, source_target_pairs={{0,1},{1,0},{2,3},{3,2},{4,5},{5,4},{6,7},{7,6},{8,9},{9,8},{10,11... | collective-permute-start | bytes 1572872 | tf_op jit(solution)/shard_map/ppermute | solution.py:221
  74.0 11.0 %shard_map.76.own = f32[128,4096]{1,0:T(8,128)S(1)} custom-call(s32[8]{0:T(128)S(1)} %copy-done.1, bf16[512,4096]{1,0:T(8,128)(2,1)S(1)} %bitcast.9, bf16[4096,1024]{1,0:T(8,128)(2,1)S(1)} %bitcast.3, bf16[512,1024]{1,0:T(8,128)(2,1)S(1)} %collective-permute-done.km, bf16[512,1024]{1,0:T(8,128)(2,1)S(1)} %collective-permute-done.1.vm, ...), custom_call_target="tpu_custom_call" | custom-call | flops 2684354560 | bytes 16777216 | tf_op jit(solution)/shard_map/pallas_call | solution.py:196
  84.9 0.0 collective-permute-done.2.xa
  85.0 0.0 collective-permute-done.7.yb
  85.0 6.7 %collective-permute-done.6.ya = bf16[128,2048]{1,0:T(8,128)(2,1)S(1)} collective-permute-done((bf16[128,2048]{1,0:T(8,128)(2,1)S(1)}, bf16[128,2048]{1,0:T(8,128)(2,1)S(1)}, u32[]{:S(2)}, u32[]{:S(2)}) %collective-permute-start.6) | collective-permute-done | bytes 524320 | tf_op jit(solution)/shard_map/ppermute | solution.py:221
  91.7 0.0 collective-permute-done.4.xb
  91.7 1.3 %shard_map.81 = bf16[1,128,4096]{2,1,0:T(8,128)(2,1)} custom-call(f32[128,4096]{1,0:T(8,128)S(1)} %shard_map.76.own, bf16[128,2048]{1,0:T(8,128)(2,1)S(1)} %collective-permute-done.2.xa, bf16[128,2048]{1,0:T(8,128)(2,1)S(1)} %collective-permute-done.4.xb, bf16[128,2048]{1,0:T(8,128)(2,1)S(1)} %collective-permute-done.6.ya, ...), custom_call_target="tpu_custom_call" | custom-call | flops 1572864 | bytes 7340032 | tf_op jit(solution)/shard_map/pallas_call | solution.py:247
  (3 shorter events, 0.0 us)
Async XLA Ops:
  0.0 9.9 %copy-start.3 = (bf16[1,512,4096]{2,1,0:T(8,128)(2,1)S(1)}, bf16[1,512,4096]{2,1,0:T(8,128)(2,1)}, u32[]{:S(2)}) copy-start(bf16[1,512,4096]{2,1,0:T(8,128)(2,1)} %param.8) | copy-start | bytes 12582916
  0.0 9.9 %copy-start.2 = (bf16[4096,1024]{1,0:T(8,128)(2,1)S(1)}, bf16[4096,1024]{1,0:T(8,128)(2,1)}, u32[]{:S(2)}) copy-start(bf16[4096,1024]{1,0:T(8,128)(2,1)} %refs_1_.1) | copy-start | bytes 25165828
  0.0 17.8 %slice-start.4 = ((s8[8388608]{0:T(1024)(128)(4,1)}), s8[4194304]{0:T(1024)(128)(4,1)S(1)}, s32[]{:S(2)}) async-start(s8[8388608]{0:T(1024)(128)(4,1)} %bitcast.10), calls=%async_computation.4 | async-start | bytes 8388608
  9.3 8.5 %copy-start = (bf16[1,512,4096]{2,1,0:T(8,128)(2,1)S(1)}, bf16[1,512,4096]{2,1,0:T(8,128)(2,1)}, u32[]{:S(2)}) copy-start(bf16[1,512,4096]{2,1,0:T(8,128)(2,1)} %param.7) | copy-start | bytes 12582916
  9.3 8.5 %slice-start.5 = ((s8[8388608]{0:T(1024)(128)(4,1)}), s8[4194304]{0:T(1024)(128)(4,1)S(1)}, s32[]{:S(2)}) async-start(s8[8388608]{0:T(1024)(128)(4,1)} %bitcast.10), calls=%async_computation.5 | async-start | bytes 8388608
  9.3 18.9 %collective-permute-start = (bf16[512,1024]{1,0:T(8,128)(2,1)S(1)}, bf16[512,1024]{1,0:T(8,128)(2,1)S(1)}, u32[]{:S(2)}, u32[]{:S(2)}) collective-permute-start(bf16[512,1024]{1,0:T(8,128)(2,1)S(1)} %shard_map.73), channel_id=1, source_target_pairs={{0,4},{4,8},{8,12},{12,16},{16,20},{20,24},{24,28},{28,0},{1,5},{5... | collective-permute-start | bytes 3145736 | tf_op jit(solution)/shard_map/ppermute | solution.py:217
  9.9 27.7 %slice-start = ((s8[8388608]{0:T(1024)(128)(4,1)}), s8[4194304]{0:T(1024)(128)(4,1)S(1)}, s32[]{:S(2)}) async-start(s8[8388608]{0:T(1024)(128)(4,1)} %bitcast.2), calls=%async_computation | async-start | bytes 8388608
  9.9 27.7 %slice-start.2 = ((s8[8388608]{0:T(1024)(128)(4,1)}), s8[4194304]{0:T(1024)(128)(4,1)S(1)}, s32[]{:S(2)}) async-start(s8[8388608]{0:T(1024)(128)(4,1)} %bitcast.4), calls=%async_computation.2 | async-start | bytes 8388608
  15.1 22.5 %collective-permute-start.1 = (bf16[512,1024]{1,0:T(8,128)(2,1)S(1)}, bf16[512,1024]{1,0:T(8,128)(2,1)S(1)}, u32[]{:S(2)}, u32[]{:S(2)}) collective-permute-start(bf16[512,1024]{1,0:T(8,128)(2,1)S(1)} %shard_map.74), channel_id=1, source_target_pairs={{0,4},{4,8},{8,12},{12,16},{16,20},{20,24},{24,28},{28,0},{1,5},{5... | collective-permute-start | bytes 3145736 | tf_op jit(solution)/shard_map/ppermute | solution.py:217
  17.8 19.8 %slice-start.1 = ((s8[8388608]{0:T(1024)(128)(4,1)}), s8[4194304]{0:T(1024)(128)(4,1)S(1)}, s32[]{:S(2)}) async-start(s8[8388608]{0:T(1024)(128)(4,1)} %bitcast.2), calls=%async_computation.1 | async-start | bytes 8388608
  17.8 19.8 %slice-start.3 = ((s8[8388608]{0:T(1024)(128)(4,1)}), s8[4194304]{0:T(1024)(128)(4,1)S(1)}, s32[]{:S(2)}) async-start(s8[8388608]{0:T(1024)(128)(4,1)} %bitcast.4), calls=%async_computation.3 | async-start | bytes 8388608
  17.8 19.8 %copy-start.1 = (s32[8]{0:T(128)S(1)}, s32[8]{0:T(128)}, u32[]{:S(2)}) copy-start(s32[8]{0:T(128)} %lens.5) | copy-start | bytes 100
  48.7 21.5 %collective-permute-start.5 = (bf16[128,2048]{1,0:T(8,128)(2,1)S(1)}, bf16[128,2048]{1,0:T(8,128)(2,1)S(1)}, u32[]{:S(2)}, u32[]{:S(2)}) collective-permute-start(bf16[128,2048]{1,0:T(8,128)(2,1)S(1)} %get-tuple-element.19), channel_id=1, source_target_pairs={{0,1},{1,0},{2,3},{3,2},{4,5},{5,4},{6,7},{7,6},{8,9},{9,8},{10,11... | collective-permute-start | bytes 1572872 | tf_op jit(solution)/shard_map/ppermute | solution.py:221
  50.7 21.6 %collective-permute-start.3 = (bf16[128,2048]{1,0:T(8,128)(2,1)S(1)}, bf16[128,2048]{1,0:T(8,128)(2,1)S(1)}, u32[]{:S(2)}, u32[]{:S(2)}) collective-permute-start(bf16[128,2048]{1,0:T(8,128)(2,1)S(1)} %get-tuple-element.17), channel_id=1, source_target_pairs={{0,2},{1,3},{2,0},{3,1},{4,6},{5,7},{6,4},{7,5},{8,10},{9,11},{10,... | collective-permute-start | bytes 1572872 | tf_op jit(solution)/shard_map/ppermute | solution.py:221
  69.5 15.5 %collective-permute-start.2 = (bf16[128,2048]{1,0:T(8,128)(2,1)S(1)}, bf16[128,2048]{1,0:T(8,128)(2,1)S(1)}, u32[]{:S(2)}, u32[]{:S(2)}) collective-permute-start(bf16[128,2048]{1,0:T(8,128)(2,1)S(1)} %get-tuple-element.15), channel_id=1, source_target_pairs={{0,1},{1,0},{2,3},{3,2},{4,5},{5,4},{6,7},{7,6},{8,9},{9,8},{10,11... | collective-permute-start | bytes 1572872 | tf_op jit(solution)/shard_map/ppermute | solution.py:221
  70.1 14.9 %collective-permute-start.7 = (bf16[128,2048]{1,0:T(8,128)(2,1)S(1)}, bf16[128,2048]{1,0:T(8,128)(2,1)S(1)}, u32[]{:S(2)}, u32[]{:S(2)}) collective-permute-start(bf16[128,2048]{1,0:T(8,128)(2,1)S(1)} %get-tuple-element.20), channel_id=1, source_target_pairs={{0,2},{1,3},{2,0},{3,1},{4,6},{5,7},{6,4},{7,5},{8,10},{9,11},{10,... | collective-permute-start | bytes 1572872 | tf_op jit(solution)/shard_map/ppermute | solution.py:221
  70.3 21.4 %collective-permute-start.6 = (bf16[128,2048]{1,0:T(8,128)(2,1)S(1)}, bf16[128,2048]{1,0:T(8,128)(2,1)S(1)}, u32[]{:S(2)}, u32[]{:S(2)}) collective-permute-start(bf16[128,2048]{1,0:T(8,128)(2,1)S(1)} %shard_map.80), channel_id=1, source_target_pairs={{0,2},{1,3},{2,0},{3,1},{4,6},{5,7},{6,4},{7,5},{8,10},{9,11},{10,... | collective-permute-start | bytes 1572872 | tf_op jit(solution)/shard_map/ppermute | solution.py:221
  72.4 19.3 %collective-permute-start.4 = (bf16[128,2048]{1,0:T(8,128)(2,1)S(1)}, bf16[128,2048]{1,0:T(8,128)(2,1)S(1)}, u32[]{:S(2)}, u32[]{:S(2)}) collective-permute-start(bf16[128,2048]{1,0:T(8,128)(2,1)S(1)} %shard_map.79), channel_id=1, source_target_pairs={{0,1},{1,0},{2,3},{3,2},{4,5},{5,4},{6,7},{7,6},{8,9},{9,8},{10,11... | collective-permute-start | bytes 1572872 | tf_op jit(solution)/shard_map/ppermute | solution.py:221

commit v2 on v1

v2 whole, which is shorter than its diff:
```python
import functools
import math

import jax
import jax.numpy as jnp
from jax import lax
from jax.experimental import pallas as pl
from jax.experimental.pallas import tpu as pltpu
from jax.sharding import PartitionSpec as P


HEAD_DIM = 128
TILE = 256
PARTS = 8
VMEM = pltpu.VMEM
BF16 = jnp.bfloat16
F32 = jnp.float32


def dot(a, b):
    return jnp.dot(a, b, preferred_element_type=F32)


def tile_of(index, size):
    return pl.ds(pl.multiple_of(index * size, size), size)


def params(limit_mib):
    return pltpu.CompilerParams(vmem_limit_bytes=limit_mib << 20)


def cost(rows, depth, cols, extra=0):
    return pl.CostEstimate(
        flops=2 * rows * depth * cols,
        bytes_accessed=2 * (rows * depth + depth * cols + rows * cols) + extra,
        transcendentals=0,
    )


def streamed_kernel(x_hbm, w_hbm, out, x, w, total, x_sem, w_sem):
    depth, cols = w_hbm.shape
    part = depth // PARTS
    copies = []
    for k in range(PARTS):
        here = pl.ds(k * part, part)
        cx = pltpu.make_async_copy(x_hbm.at[:, here], x.at[:, here], x_sem.at[k])
        cw = pltpu.make_async_copy(w_hbm.at[here, :], w.at[here, :], w_sem.at[k])
        cx.start()
        cw.start()
        copies.append((cx, cw))
    for k in range(PARTS):
        copies[k][0].wait()
        copies[k][1].wait()
        here = pl.ds(k * part, part)
        for j in range(cols // TILE):
            lanes = pl.ds(j * TILE, TILE)
            term = dot(x[:, here], w[here, lanes])
            if k > 0:
                term = total[:, lanes] + term
            if k < PARTS - 1:
                total[:, lanes] = term
            else:
                out[:, lanes] = term.astype(BF16)


def streamed(x, w):
    rows, depth = x.shape
    cols = w.shape[1]
    return pl.pallas_call(
        streamed_kernel,
        out_shape=[jax.ShapeDtypeStruct(s, BF16) for s in ((rows, cols), x.shape, w.shape)],
        in_specs=[pl.BlockSpec(memory_space=pltpu.HBM)] * 2,
        out_specs=[pl.BlockSpec(memory_space=VMEM)] * 3,
        scratch_shapes=[
            VMEM((rows, cols), F32),
            pltpu.SemaphoreType.DMA((PARTS,)),
            pltpu.SemaphoreType.DMA((PARTS,)),
        ],
        compiler_params=params(4),
        cost_estimate=cost(rows, depth, cols),
    )(*(pltpu.with_memory_space_constraint(a, pltpu.HBM) for a in (x, w)))


def resident_kernel(count, x, *refs):
    cols = refs[0].shape[1]
    for w, out in zip(refs[:count], refs[count:]):

        def step(j, carry, w=w, out=out):
            out[:, tile_of(j, TILE)] = dot(x[...], w[:, tile_of(j, TILE)]).astype(BF16)
            return carry

        lax.fori_loop(0, cols // TILE, step, 0)


def resident(x, *ws):
    rows, depth = x.shape
    cols = ws[0].shape[1]
    count = len(ws)
    out = pl.pallas_call(
        functools.partial(resident_kernel, count),
        out_shape=[jax.ShapeDtypeStruct((rows, cols), BF16)] * count,
        in_specs=[pl.BlockSpec(memory_space=VMEM)] * (1 + count),
        out_specs=[pl.BlockSpec(memory_space=VMEM)] * count,
        compiler_params=params(4),
        cost_estimate=cost(rows, depth, cols * count),
    )(x, *ws)
    return out


def block_rows(b, rows):
    return pl.ds(b * rows, rows) if isinstance(b, int) else tile_of(b, rows)


def weigh_kernel(blocks_of, lens, q, km, ko, p, bias):
    blocks = blocks_of()
    width = q.shape[1]
    keys = ko.shape[0]
    rows = p.shape[1] // len(blocks)
    group = lax.axis_index("seq")
    total = lens.shape[0]
    own_len = lens[group]
    mem_len = lens[lax.rem(group + total - 1, total)]
    scale = math.log2(math.e) / math.sqrt(HEAD_DIM)
    nt = (((1,), (1,)), ((), ()))
    mem_cols, own_cols = pl.ds(0, keys), pl.ds(keys, keys)
    col = lax.broadcasted_iota(jnp.int32, (rows, keys), 1)
    bias[:, mem_cols] = jnp.where(col < mem_len, 0.0, -1e30)
    for n, b in enumerate(blocks):
        here = pl.ds(n * rows, rows)
        row = lax.broadcasted_iota(jnp.int32, (rows, keys), 0) + b * rows
        bias[:, own_cols] = jnp.where((col <= row) & (col < own_len), 0.0, -1e30)
        for h in range(width // HEAD_DIM):
            lanes = pl.ds(h * HEAD_DIM, HEAD_DIM)
            one = q[block_rows(b, rows), lanes]
            sm = lax.dot_general(one, km[:, lanes], nt, preferred_element_type=F32)
            so = lax.dot_general(one, ko[:, lanes], nt, preferred_element_type=F32)
            sm = sm + bias[:, mem_cols]
            so = so + bias[:, own_cols]
            top = jnp.maximum(
                jnp.max(sm, axis=-1, keepdims=True), jnp.max(so, axis=-1, keepdims=True)
            )
            pm = jnp.exp2((sm - top) * scale)
            po = jnp.exp2((so - top) * scale)
            norm = jnp.sum(pm, axis=-1, keepdims=True) + jnp.sum(po, axis=-1, keepdims=True)
            inverse = 1.0 / norm
            p[h, here, mem_cols] = (pm * inverse).astype(BF16)
            p[h, here, own_cols] = (po * inverse).astype(BF16)


def weigh(blocks_of, count, rows, lens, q, km, ko):
    width = q.shape[1]
    keys = ko.shape[0]
    heads = width // HEAD_DIM
    return pl.pallas_call(
        functools.partial(weigh_kernel, blocks_of),
        out_shape=jax.ShapeDtypeStruct((heads, count * rows, 2 * keys), BF16),
        in_specs=[pl.BlockSpec(memory_space=pltpu.SMEM)] + [pl.BlockSpec(memory_space=VMEM)] * 3,
        out_specs=pl.BlockSpec(memory_space=VMEM),
        scratch_shapes=[VMEM((rows, 2 * keys), F32)],
        compiler_params=params(8),
        cost_estimate=pl.CostEstimate(
            flops=4 * count * rows * width * keys,
            bytes_accessed=0,
            transcendentals=heads * count * rows * 2 * keys,
        ),
    )(lens, q, km, ko)


def attend_kernel(first, count, split, p, vm, vo, wo, *refs):
    outs = refs[: len(split)]
    (ctx,) = refs[len(split) :]
    rows = ctx.shape[0] // count
    keys, width = vo.shape
    here = pl.ds(first * rows, count * rows)
    for h in range(width // HEAD_DIM):
        lanes = pl.ds(h * HEAD_DIM, HEAD_DIM)
        mixed = dot(p[h, here, pl.ds(0, keys)], vm[:, lanes])
        mixed = mixed + dot(p[h, here, pl.ds(keys, keys)], vo[:, lanes])
        ctx[:, lanes] = mixed.astype(BF16)
    wide = 2 * TILE
    for j in range(wo.shape[1] // wide):
        term = dot(ctx[...], wo[:, pl.ds(j * wide, wide)])
        for out, (block, start, size) in zip(outs, split):
            if start <= j * wide < start + size:
                part = term[block * rows : (block + 1) * rows]
                out[:, pl.ds(j * wide - start, wide)] = part.astype(out.dtype)


def attend(first, count, split, kinds, rows, p, vm, vo, wo):
    keys, width = vo.shape
    depth = wo.shape[1]
    return pl.pallas_call(
        functools.partial(attend_kernel, first, count, split),
        out_shape=[
            jax.ShapeDtypeStruct((rows, cols), kind) for (_, _, cols), kind in zip(split, kinds)
        ],
        in_specs=[pl.BlockSpec(memory_space=VMEM)] * 4,
        out_specs=[pl.BlockSpec(memory_space=VMEM)] * len(split),
        scratch_shapes=[VMEM((count * rows, width), BF16)],
        compiler_params=params(8),
        cost_estimate=pl.CostEstimate(
            flops=2 * count * rows * width * (depth + 2 * keys),
            bytes_accessed=2 * depth * width,
            transcendentals=0,
        ),
    )(p, vm, vo, wo)


def shifted(x):
    devices = lax.axis_size("seq")
    return lax.ppermute(x, "seq", [(i, (i + 1) % devices) for i in range(devices)])


def swapped(x, bit):
    return lax.ppermute(x, "tp", [(i, i ^ bit) for i in range(lax.axis_size("tp"))])


def add_kernel(a, b, out):
    out[...] = (a[...] + b[...].astype(F32)).astype(BF16)


def add(a, b):
    return pl.pallas_call(
        add_kernel,
        out_shape=jax.ShapeDtypeStruct(a.shape, BF16),
        in_specs=[pl.BlockSpec(memory_space=VMEM)] * 2,
        out_specs=pl.BlockSpec(memory_space=VMEM),
        compiler_params=params(4),
        cost_estimate=pl.CostEstimate(flops=a.size, bytes_accessed=8 * a.size, transcendentals=0),
    )(a, b)


def final_kernel(own, xa, xb, ya, yb, out):
    half = xa.shape[1]
    left, right = pl.ds(0, half), pl.ds(half, half)
    out[0, :, left] = (own[:, left] + xa[...].astype(F32) + ya[...].astype(F32)).astype(BF16)
    out[0, :, right] = (own[:, right] + xb[...].astype(F32) + yb[...].astype(F32)).astype(BF16)


def final(own, *parts):
    return pl.pallas_call(
        final_kernel,
        out_shape=jax.ShapeDtypeStruct((1, *own.shape), BF16),
        in_specs=[pl.BlockSpec(memory_space=VMEM)] * 5,
        out_specs=pl.BlockSpec(memory_space=VMEM),
        compiler_params=params(4),
        cost_estimate=pl.CostEstimate(
            flops=3 * own.size, bytes_accessed=14 * own.size, transcendentals=0
        ),
    )(own, *parts)


def body(layer_input, memory, lens, wq, wk, wv, wo):
    seg_rows = layer_input.shape[1]
    shares = lax.axis_size("tp")
    x = layer_input[0]
    rows = seg_rows // shares
    half = wo.shape[1] // 2
    sent_keys, near_memory, near_wk = streamed(memory[0], wk)
    mem_keys = shifted(sent_keys)
    (sent_values,) = resident(near_memory, wv)
    mem_values = shifted(sent_values)
    own_keys, own_values, queries = resident(x, near_wk, wv, wq)
    sides = (lens, queries, mem_keys, own_keys)
    tail = (mem_values, own_values, wo)
    whole = (0, 2 * half)
    if shares != 4:
        p = weigh(lambda: list(range(shares)), shares, rows, *sides)
        split = tuple((b, *whole) for b in range(shares))
        terms = attend(0, shares, split, (F32,) * shares, rows, p, *tail)
        summed = lax.psum_scatter(
            jnp.concatenate(terms), "tp", scatter_dimension=0, tiled=True
        )
        return summed.astype(BF16)[None]

    def far():
        return [lax.axis_index("tp") ^ 3]

    def others():
        return [lax.axis_index("tp") ^ 1, lax.axis_index("tp") ^ 2, lax.axis_index("tp")]

    p_far = weigh(far, 1, rows, *sides)
    lower, upper = (0, half), (half, half)
    far_a, far_b = attend(0, 1, ((0, *lower), (0, *upper)), (BF16, BF16), rows, p_far, *tail)
    got_a, got_b = swapped(far_a, 1), swapped(far_b, 2)
    p_rest = weigh(others, 3, rows, *sides)
    split = ((0, *lower), (0, *upper), (1, *lower), (1, *upper))
    xa, xb, ya, yb = attend(0, 2, split, (BF16, F32, F32, BF16), rows, p_rest, *tail)
    from_xa, from_yb = swapped(xa, 1), swapped(yb, 2)
    from_xb, from_ya = swapped(add(xb, got_b), 1), swapped(add(ya, got_a), 2)
    (own,) = attend(2, 1, ((0, *whole),), (F32,), rows, p_rest, *tail)
    return final(own, from_xa, from_xb, from_ya, from_yb)


def solution(mesh):
    return jax.shard_map(
        body,
        mesh=mesh,
        in_specs=(
            P("seq", None, None),
            P("seq", None, None),
            P(),
            P(None, "tp"),
            P(None, "tp"),
            P(None, "tp"),
            P("tp", None),
        ),
        out_specs=P("seq", "tp", None),
        check_vma=False,
    )
```

time: 93.2 us -> 81.6 us (0.88)
  Pallas kernels: 65.5 us -> 43.7 us
  waiting for transfers between devices: 16.2 us -> 26.1 us
    pallas_call x4 -> x6, Pallas kernels: 48.5 us -> 21.4 us  [the longest x2 7.55 us: weigh(): pl.pallas_call(functools.partial(weigh_kernel, blocks_of), out_shape=jax....]
    ppermute x6, waiting for transfers between devices: 6.76 us -> 16.8 us  [swapped(): lax.ppermute(x, 'tp', [(i, i ^ bit) for i in range(lax.axis_size('tp'))])]
    pallas_call x2, Pallas kernels: 15.5 us -> 20.8 us  [resident(): pl.pallas_call(functools.partial(resident_kernel, count), out_shape=[jax....]
  transfers between devices with their start and end apart: 8 -> 8, of which waited for: 2 -> 4; matrix products, arithmetic and copies ran while one was open for 0% -> 0% of each run, Pallas kernels for 47% -> 35%
where the time goes in v2:
time: 81.6 us; the launch traced here: 81.5 us
  Pallas kernels  43.7 us (54%)
  waiting for transfers between devices  26.1 us (32%)
  starting transfers between devices  11 us (13%)
    pallas_call x2, Pallas kernels, resident(): pl.pallas_call(functools.partial(resident_kernel, count), out_shape=[jax....  20.8 us
    ppermute x6, waiting for transfers between devices, swapped(): lax.ppermute(x, 'tp', [(i, i ^ bit) for i in range(lax.axis_size('tp'))])  16.8 us
    ppermute x2, waiting for transfers between devices, shifted(): lax.ppermute(x, 'seq', [(i, (i + 1) % devices) for i in range(devices)])  9.34 us
    ppermute x6, starting transfers between devices, swapped(): lax.ppermute(x, 'tp', [(i, i ^ bit) for i in range(lax.axis_size('tp'))])  7.82 us
    pallas_call x2, Pallas kernels, weigh(): pl.pallas_call(functools.partial(weigh_kernel, blocks_of), out_shape=jax....  7.55 us
    pallas_call x3, Pallas kernels, attend(): pl.pallas_call(functools.partial(attend_kernel, first, count, split), out...  7.23 us
    pallas_call x1, Pallas kernels, streamed(): pl.pallas_call(streamed_kernel, out_shape=[jax.ShapeDtypeStruct(s, BF16)...  6.63 us
    ppermute x2, starting transfers between devices, shifted(): lax.ppermute(x, 'seq', [(i, (i + 1) % devices) for i in range(devices)])  3.22 us
  transfers between devices with their start and end apart: 8, of which 4 were waited for; matrix products, arithmetic and copies ran while one was open for 0% of the time, Pallas kernels for 35%

profile of v2, /device:TPU:0, one launch (start us, length us, event | category | flops | bytes accessed | tf_op | source)
XLA Modules:
  0.0 81.5 jit_solution(6797746729245678868)
XLA Ops:
  0.0 0.0 copy-start.1
  0.0 0.0 slice-start.2
  0.0 6.6 %shard_map.73 = (bf16[512,1024]{1,0:T(8,128)(2,1)S(1)}, bf16[512,4096]{1,0:T(8,128)(2,1)S(1)}, bf16[4096,1024]{1,0:T(8,128)(2,1)S(1)}) custom-call(bf16[512,4096]{1,0:T(8,128)(2,1)} %bitcast.7, bf16[4096,1024]{1,0:T(8,128)(2,1)} %w_hbm.1), custom_call_target="tpu_custom_call" | custom-call | flops 4294967296 | bytes 13631488 | tf_op jit(solution)/shard_map/pallas_call | solution.py:69
  6.6 0.4 copy-done.1
  7.1 0.0 slice-start.3
  7.1 0.0 copy-start.2
  7.1 5.2 %shard_map.76 = bf16[512,1024]{1,0:T(8,128)(2,1)S(1)} custom-call(bf16[512,4096]{1,0:T(8,128)(2,1)S(1)} %get-tuple-element.21.x, bf16[4096,1024]{1,0:T(8,128)(2,1)S(1)} %copy-done.1), custom_call_target="tpu_custom_call" | custom-call | flops 4294967296 | bytes 13631488 | tf_op jit(solution)/shard_map/pallas_call | solution.py:99
  12.3 0.5 collective-permute-start.1
  12.8 2.7 %collective-permute-start = (bf16[512,1024]{1,0:T(8,128)(2,1)S(1)}, bf16[512,1024]{1,0:T(8,128)(2,1)S(1)}, u32[]{:S(2)}, u32[]{:S(2)}) collective-permute-start(bf16[512,1024]{1,0:T(8,128)(2,1)S(1)} %get-tuple-element.19), channel_id=1, source_target_pairs={{0,4},{4,8},{8,12},{12,16},{16,20},{20,24},{24,28},{28,0},{1,5},{5... | collective-permute-start | bytes 3145736 | tf_op jit(solution)/shard_map/ppermute | solution.py:211
  15.5 0.0 slice-start
  15.5 0.0 slice-done.2
  15.5 0.0 slice-done.3
  15.5 0.0 copy-done.2
  15.5 0.0 copy-start
  15.5 0.0 slice-start.1
  15.5 15.7 %shard_map.74 = (bf16[512,1024]{1,0:T(8,128)(2,1)S(1)}, bf16[512,1024]{1,0:T(8,128)(2,1)S(1)}, bf16[512,1024]{1,0:T(8,128)(2,1)S(1)}) custom-call(bf16[512,4096]{1,0:T(8,128)(2,1)S(1)} %bitcast.6, bf16[4096,1024]{1,0:T(8,128)(2,1)S(1)} %get-tuple-element.17.refs_0_, bf16[4096,1024]{1,0:T(8,128)(2,1)S(1)} %copy-done.1, bf16[4096,1024]{1,0:T(8,128)(2,1)S(1)} %bitcast.5), custom_call_target="tpu_custom_call" | custom-call | flops 12884901888 | bytes 32505856 | tf_op jit(solution)/shard_map/pallas_call | solution.py:99
  31.2 9.3 %collective-permute-done.km = bf16[512,1024]{1,0:T(8,128)(2,1)S(1)} collective-permute-done((bf16[512,1024]{1,0:T(8,128)(2,1)S(1)}, bf16[512,1024]{1,0:T(8,128)(2,1)S(1)}, u32[]{:S(2)}, u32[]{:S(2)}) %collective-permute-start) | collective-permute-done | bytes 1048608 | tf_op jit(solution)/shard_map/ppermute | solution.py:211
  40.5 0.0 copy-done
  40.6 2.2 %shard_map.79.p = bf16[8,128,1024]{2,1,0:T(8,128)(2,1)S(1)} custom-call(s32[8]{0:T(128)S(1)} %copy-done, bf16[512,1024]{1,0:T(8,128)(2,1)S(1)} %get-tuple-element.18.q, bf16[512,1024]{1,0:T(8,128)(2,1)S(1)} %collective-permute-done.km, bf16[512,1024]{1,0:T(8,128)(2,1)S(1)} %get-tuple-element.20.ko), custom_call_target="tpu_custom_call" | custom-call | flops 268435456 | tf_op jit(solution)/shard_map/pallas_call | solution.py:154
  42.7 0.0 collective-permute-done.1.vm
  42.8 0.0 slice-done
  42.8 0.0 slice-done.1
  42.8 1.9 %shard_map.80 = (bf16[128,2048]{1,0:T(8,128)(2,1)S(1)}, bf16[128,2048]{1,0:T(8,128)(2,1)S(1)}) custom-call(bf16[8,128,1024]{2,1,0:T(8,128)(2,1)S(1)} %shard_map.79.p, bf16[512,1024]{1,0:T(8,128)(2,1)S(1)} %collective-permute-done.1.vm, bf16[512,1024]{1,0:T(8,128)(2,1)S(1)} %get-tuple-element.22.vo, bf16[1024,4096]{1,0:T(8,128)(2,1)S(1)} %bitcast.3), custom_call_target="tpu_custom_call" | custom-call | flops 1342177280 | bytes 8388608 | tf_op jit(solution)/shard_map/pallas_call | solution.py:192
  44.7 2.1 %collective-permute-start.3 = (bf16[128,2048]{1,0:T(8,128)(2,1)S(1)}, bf16[128,2048]{1,0:T(8,128)(2,1)S(1)}, u32[]{:S(2)}, u32[]{:S(2)}) collective-permute-start(bf16[128,2048]{1,0:T(8,128)(2,1)S(1)} %get-tuple-element.25), channel_id=1, source_target_pairs={{0,2},{1,3},{2,0},{3,1},{4,6},{5,7},{6,4},{7,5},{8,10},{9,11},{10,... | collective-permute-start | bytes 1572872 | tf_op jit(solution)/shard_map/ppermute | solution.py:215
  46.8 1.5 %collective-permute-start.5 = (bf16[128,2048]{1,0:T(8,128)(2,1)S(1)}, bf16[128,2048]{1,0:T(8,128)(2,1)S(1)}, u32[]{:S(2)}, u32[]{:S(2)}) collective-permute-start(bf16[128,2048]{1,0:T(8,128)(2,1)S(1)} %get-tuple-element.27), channel_id=1, source_target_pairs={{0,1},{1,0},{2,3},{3,2},{4,5},{5,4},{6,7},{7,6},{8,9},{9,8},{10,11... | collective-permute-start | bytes 1572872 | tf_op jit(solution)/shard_map/ppermute | solution.py:215
  48.3 5.4 %shard_map.75.p = bf16[8,384,1024]{2,1,0:T(8,128)(2,1)S(1)} custom-call(s32[8]{0:T(128)S(1)} %copy-done, bf16[512,1024]{1,0:T(8,128)(2,1)S(1)} %get-tuple-element.18.q, bf16[512,1024]{1,0:T(8,128)(2,1)S(1)} %collective-permute-done.km, bf16[512,1024]{1,0:T(8,128)(2,1)S(1)} %get-tuple-element.20.ko), custom_call_target="tpu_custom_call" | custom-call | flops 805306368 | tf_op jit(solution)/shard_map/pallas_call | solution.py:154
  53.7 3.4 %shard_map.78 = (bf16[128,2048]{1,0:T(8,128)(2,1)S(1)}, f32[128,2048]{1,0:T(8,128)S(1)}, f32[128,2048]{1,0:T(8,128)S(1)}, bf16[128,2048]{1,0:T(8,128)(2,1)S(1)}) custom-call(bf16[8,384,1024]{2,1,0:T(8,128)(2,1)S(1)} %shard_map.75.p, bf16[512,1024]{1,0:T(8,128)(2,1)S(1)} %collective-permute-done.1.vm, bf16[512,1024]{1,0:T(8,128)(2,1)S(1)} %get-tuple-element.22.vo, ...), custom_call_target="tpu_custom_call" | custom-call | flops 2684354560 | bytes 8388608 | tf_op jit(solution)/shard_map/pallas_call | solution.py:192
  57.1 0.6 collective-permute-start.2
  57.7 0.1 collective-permute-start.7
  57.8 0.0 collective-permute-done.3.b
  57.8 0.1 shard_map.81
  57.9 2.0 %collective-permute-start.4 = (bf16[128,2048]{1,0:T(8,128)(2,1)S(1)}, bf16[128,2048]{1,0:T(8,128)(2,1)S(1)}, u32[]{:S(2)}, u32[]{:S(2)}) collective-permute-start(bf16[128,2048]{1,0:T(8,128)(2,1)S(1)} %shard_map.81), channel_id=1, source_target_pairs={{0,1},{1,0},{2,3},{3,2},{4,5},{5,4},{6,7},{7,6},{8,9},{9,8},{10,11... | collective-permute-start | bytes 1572872 | tf_op jit(solution)/shard_map/ppermute | solution.py:215
  59.9 0.0 collective-permute-done.5.b
  59.9 0.1 shard_map.82
  60.0 1.6 %collective-permute-start.6 = (bf16[128,2048]{1,0:T(8,128)(2,1)S(1)}, bf16[128,2048]{1,0:T(8,128)(2,1)S(1)}, u32[]{:S(2)}, u32[]{:S(2)}) collective-permute-start(bf16[128,2048]{1,0:T(8,128)(2,1)S(1)} %shard_map.82), channel_id=1, source_target_pairs={{0,2},{1,3},{2,0},{3,1},{4,6},{5,7},{6,4},{7,5},{8,10},{9,11},{10,... | collective-permute-start | bytes 1572872 | tf_op jit(solution)/shard_map/ppermute | solution.py:215
  61.6 1.9 %shard_map.77.own = f32[128,4096]{1,0:T(8,128)S(1)} custom-call(bf16[8,384,1024]{2,1,0:T(8,128)(2,1)S(1)} %shard_map.75.p, bf16[512,1024]{1,0:T(8,128)(2,1)S(1)} %collective-permute-done.1.vm, bf16[512,1024]{1,0:T(8,128)(2,1)S(1)} %get-tuple-element.22.vo, bf16[1024,4096]{1,0:T(8,128)(2,1)S(1)} %bitcast.3), custom_call_target="tpu_custom_call" | custom-call | flops 1342177280 | bytes 8388608 | tf_op jit(solution)/shard_map/pallas_call | solution.py:192
  63.4 8.5 %collective-permute-done.2.xa = bf16[128,2048]{1,0:T(8,128)(2,1)S(1)} collective-permute-done((bf16[128,2048]{1,0:T(8,128)(2,1)S(1)}, bf16[128,2048]{1,0:T(8,128)(2,1)S(1)}, u32[]{:S(2)}, u32[]{:S(2)}) %collective-permute-start.2) | collective-permute-done | bytes 524320 | tf_op jit(solution)/shard_map/ppermute | solution.py:215
  72.0 0.5 collective-permute-done.7.yb
  72.5 7.7 %collective-permute-done.4.xb = bf16[128,2048]{1,0:T(8,128)(2,1)S(1)} collective-permute-done((bf16[128,2048]{1,0:T(8,128)(2,1)S(1)}, bf16[128,2048]{1,0:T(8,128)(2,1)S(1)}, u32[]{:S(2)}, u32[]{:S(2)}) %collective-permute-start.4) | collective-permute-done | bytes 524320 | tf_op jit(solution)/shard_map/ppermute | solution.py:215
  80.2 0.0 collective-permute-done.6.ya
  80.2 1.3 %shard_map.83 = bf16[1,128,4096]{2,1,0:T(8,128)(2,1)} custom-call(f32[128,4096]{1,0:T(8,128)S(1)} %shard_map.77.own, bf16[128,2048]{1,0:T(8,128)(2,1)S(1)} %collective-permute-done.2.xa, bf16[128,2048]{1,0:T(8,128)(2,1)S(1)} %collective-permute-done.4.xb, bf16[128,2048]{1,0:T(8,128)(2,1)S(1)} %collective-permute-done.6.ya, ...), custom_call_target="tpu_custom_call" | custom-call | flops 1572864 | bytes 7340032 | tf_op jit(solution)/shard_map/pallas_call | solution.py:241
  (2 shorter events, 0.0 us)
Async XLA Ops:
  0.0 7.1 %copy-start.1 = (bf16[4096,1024]{1,0:T(8,128)(2,1)S(1)}, bf16[4096,1024]{1,0:T(8,128)(2,1)}, u32[]{:S(2)}) copy-start(bf16[4096,1024]{1,0:T(8,128)(2,1)} %refs_0_.1) | copy-start | bytes 25165828
  0.0 15.5 %slice-start.2 = ((s8[8388608]{0:T(1024)(128)(4,1)}), s8[4194304]{0:T(1024)(128)(4,1)S(1)}, s32[]{:S(2)}) async-start(s8[8388608]{0:T(1024)(128)(4,1)} %bitcast.4), calls=%async_computation.2 | async-start | bytes 8388608
  7.1 8.4 %slice-start.3 = ((s8[8388608]{0:T(1024)(128)(4,1)}), s8[4194304]{0:T(1024)(128)(4,1)S(1)}, s32[]{:S(2)}) async-start(s8[8388608]{0:T(1024)(128)(4,1)} %bitcast.4), calls=%async_computation.3 | async-start | bytes 8388608
  7.1 8.4 %copy-start.2 = (bf16[1,512,4096]{2,1,0:T(8,128)(2,1)S(1)}, bf16[1,512,4096]{2,1,0:T(8,128)(2,1)}, u32[]{:S(2)}) copy-start(bf16[1,512,4096]{2,1,0:T(8,128)(2,1)} %param.7) | copy-start | bytes 12582916
  12.3 30.5 %collective-permute-start.1 = (bf16[512,1024]{1,0:T(8,128)(2,1)S(1)}, bf16[512,1024]{1,0:T(8,128)(2,1)S(1)}, u32[]{:S(2)}, u32[]{:S(2)}) collective-permute-start(bf16[512,1024]{1,0:T(8,128)(2,1)S(1)} %shard_map.76), channel_id=1, source_target_pairs={{0,4},{4,8},{8,12},{12,16},{16,20},{20,24},{24,28},{28,0},{1,5},{5... | collective-permute-start | bytes 3145736 | tf_op jit(solution)/shard_map/ppermute | solution.py:211
  12.8 27.7 %collective-permute-start = (bf16[512,1024]{1,0:T(8,128)(2,1)S(1)}, bf16[512,1024]{1,0:T(8,128)(2,1)S(1)}, u32[]{:S(2)}, u32[]{:S(2)}) collective-permute-start(bf16[512,1024]{1,0:T(8,128)(2,1)S(1)} %get-tuple-element.19), channel_id=1, source_target_pairs={{0,4},{4,8},{8,12},{12,16},{16,20},{20,24},{24,28},{28,0},{1,5},{5... | collective-permute-start | bytes 3145736 | tf_op jit(solution)/shard_map/ppermute | solution.py:211
  15.5 27.3 %slice-start = ((s8[8388608]{0:T(1024)(128)(4,1)}), s8[4194304]{0:T(1024)(128)(4,1)S(1)}, s32[]{:S(2)}) async-start(s8[8388608]{0:T(1024)(128)(4,1)} %bitcast.2), calls=%async_computation | async-start | bytes 8388608
  15.5 25.1 %copy-start = (s32[8]{0:T(128)S(1)}, s32[8]{0:T(128)}, u32[]{:S(2)}) copy-start(s32[8]{0:T(128)} %lens.3) | copy-start | bytes 100
  15.5 27.3 %slice-start.1 = ((s8[8388608]{0:T(1024)(128)(4,1)}), s8[4194304]{0:T(1024)(128)(4,1)S(1)}, s32[]{:S(2)}) async-start(s8[8388608]{0:T(1024)(128)(4,1)} %bitcast.2), calls=%async_computation.1 | async-start | bytes 8388608
  44.7 13.1 %collective-permute-start.3 = (bf16[128,2048]{1,0:T(8,128)(2,1)S(1)}, bf16[128,2048]{1,0:T(8,128)(2,1)S(1)}, u32[]{:S(2)}, u32[]{:S(2)}) collective-permute-start(bf16[128,2048]{1,0:T(8,128)(2,1)S(1)} %get-tuple-element.25), channel_id=1, source_target_pairs={{0,2},{1,3},{2,0},{3,1},{4,6},{5,7},{6,4},{7,5},{8,10},{9,11},{10,... | collective-permute-start | bytes 1572872 | tf_op jit(solution)/shard_map/ppermute | solution.py:215
  46.8 13.1 %collective-permute-start.5 = (bf16[128,2048]{1,0:T(8,128)(2,1)S(1)}, bf16[128,2048]{1,0:T(8,128)(2,1)S(1)}, u32[]{:S(2)}, u32[]{:S(2)}) collective-permute-start(bf16[128,2048]{1,0:T(8,128)(2,1)S(1)} %get-tuple-element.27), channel_id=1, source_target_pairs={{0,1},{1,0},{2,3},{3,2},{4,5},{5,4},{6,7},{7,6},{8,9},{9,8},{10,11... | collective-permute-start | bytes 1572872 | tf_op jit(solution)/shard_map/ppermute | solution.py:215
  57.1 14.9 %collective-permute-start.2 = (bf16[128,2048]{1,0:T(8,128)(2,1)S(1)}, bf16[128,2048]{1,0:T(8,128)(2,1)S(1)}, u32[]{:S(2)}, u32[]{:S(2)}) collective-permute-start(bf16[128,2048]{1,0:T(8,128)(2,1)S(1)} %get-tuple-element.23), channel_id=1, source_target_pairs={{0,1},{1,0},{2,3},{3,2},{4,5},{5,4},{6,7},{7,6},{8,9},{9,8},{10,11... | collective-permute-start | bytes 1572872 | tf_op jit(solution)/shard_map/ppermute | solution.py:215
  57.7 14.8 %collective-permute-start.7 = (bf16[128,2048]{1,0:T(8,128)(2,1)S(1)}, bf16[128,2048]{1,0:T(8,128)(2,1)S(1)}, u32[]{:S(2)}, u32[]{:S(2)}) collective-permute-start(bf16[128,2048]{1,0:T(8,128)(2,1)S(1)} %get-tuple-element.28), channel_id=1, source_target_pairs={{0,2},{1,3},{2,0},{3,1},{4,6},{5,7},{6,4},{7,5},{8,10},{9,11},{10,... | collective-permute-start | bytes 1572872 | tf_op jit(solution)/shard_map/ppermute | solution.py:215
  57.9 22.3 %collective-permute-start.4 = (bf16[128,2048]{1,0:T(8,128)(2,1)S(1)}, bf16[128,2048]{1,0:T(8,128)(2,1)S(1)}, u32[]{:S(2)}, u32[]{:S(2)}) collective-permute-start(bf16[128,2048]{1,0:T(8,128)(2,1)S(1)} %shard_map.81), channel_id=1, source_target_pairs={{0,1},{1,0},{2,3},{3,2},{4,5},{5,4},{6,7},{7,6},{8,9},{9,8},{10,11... | collective-permute-start | bytes 1572872 | tf_op jit(solution)/shard_map/ppermute | solution.py:215
  60.0 20.2 %collective-permute-start.6 = (bf16[128,2048]{1,0:T(8,128)(2,1)S(1)}, bf16[128,2048]{1,0:T(8,128)(2,1)S(1)}, u32[]{:S(2)}, u32[]{:S(2)}) collective-permute-start(bf16[128,2048]{1,0:T(8,128)(2,1)S(1)} %shard_map.82), channel_id=1, source_target_pairs={{0,2},{1,3},{2,0},{3,1},{4,6},{5,7},{6,4},{7,5},{8,10},{9,11},{10,... | collective-permute-start | bytes 1572872 | tf_op jit(solution)/shard_map/ppermute | solution.py:215

commit v3 on v2

v3 whole, which is shorter than its diff:
```python
import functools
import math

import jax
import jax.numpy as jnp
from jax import lax
from jax.experimental import pallas as pl
from jax.experimental.pallas import tpu as pltpu
from jax.sharding import PartitionSpec as P


HEAD_DIM = 128
TILE = 256
PARTS = 8
VMEM = pltpu.VMEM
BF16 = jnp.bfloat16
F32 = jnp.float32


def dot(a, b):
    return jnp.dot(a, b, preferred_element_type=F32)


def tile_of(index, size):
    return pl.ds(pl.multiple_of(index * size, size), size)


def params(limit_mib):
    return pltpu.CompilerParams(vmem_limit_bytes=limit_mib << 20)


def cost(rows, depth, cols, extra=0):
    return pl.CostEstimate(
        flops=2 * rows * depth * cols,
        bytes_accessed=2 * (rows * depth + depth * cols + rows * cols) + extra,
        transcendentals=0,
    )


def streamed_kernel(start, x_hbm, w_hbm, out, w, *refs):
    depth, cols = w.shape
    part = depth // PARTS
    if len(refs) == 4:
        x, total, w_sem, x_sem = refs
    else:
        (total, w_sem), x, x_sem = refs, x_hbm, None
    copies = []
    for k in range(PARTS):
        here = pl.ds(k * part, part)
        source = w_hbm.at[here, pl.ds(start, cols)]
        both = [pltpu.make_async_copy(source, w.at[here, :], w_sem.at[k])]
        if x_sem is not None:
            both.append(pltpu.make_async_copy(x_hbm.at[:, here], x.at[:, here], x_sem.at[k]))
        for copy in both:
            copy.start()
        copies.append(both)
    for k in range(PARTS):
        for copy in copies[k]:
            copy.wait()
        here = pl.ds(k * part, part)
        for j in range(cols // TILE):
            lanes = pl.ds(j * TILE, TILE)
            term = dot(x[:, here], w[here, lanes])
            if k > 0:
                term = total[:, lanes] + term
            if k < PARTS - 1:
                total[:, lanes] = term
            else:
                out[:, lanes] = term.astype(BF16)


def streamed(x, w, start, cols, from_hbm):
    rows, depth = x.shape
    outs = ((rows, cols), (depth, cols)) + ((x.shape,) if from_hbm else ())
    space = pltpu.HBM if from_hbm else VMEM
    sems = [pltpu.SemaphoreType.DMA((PARTS,))] * (2 if from_hbm else 1)
    return pl.pallas_call(
        functools.partial(streamed_kernel, start),
        out_shape=[jax.ShapeDtypeStruct(s, BF16) for s in outs],
        in_specs=[pl.BlockSpec(memory_space=space), pl.BlockSpec(memory_space=pltpu.HBM)],
        out_specs=[pl.BlockSpec(memory_space=VMEM)] * len(outs),
        scratch_shapes=[VMEM((rows, cols), F32)] + sems,
        compiler_params=params(4),
        cost_estimate=cost(rows, depth, cols),
    )(
        pltpu.with_memory_space_constraint(x, pltpu.HBM) if from_hbm else x,
        pltpu.with_memory_space_constraint(w, pltpu.HBM),
    )


def resident_kernel(count, x, *refs):
    cols = refs[0].shape[1]
    for w, out in zip(refs[:count], refs[count:]):

        def step(j, carry, w=w, out=out):
            out[:, tile_of(j, TILE)] = dot(x[...], w[:, tile_of(j, TILE)]).astype(BF16)
            return carry

        lax.fori_loop(0, cols // TILE, step, 0)


def resident(x, *ws):
    rows, depth = x.shape
    cols = ws[0].shape[1]
    count = len(ws)
    out = pl.pallas_call(
        functools.partial(resident_kernel, count),
        out_shape=[jax.ShapeDtypeStruct((rows, cols), BF16)] * count,
        in_specs=[pl.BlockSpec(memory_space=VMEM)] * (1 + count),
        out_specs=[pl.BlockSpec(memory_space=VMEM)] * count,
        compiler_params=params(4),
        cost_estimate=cost(rows, depth, cols * count),
    )(x, *ws)
    return out


def block_rows(b, rows):
    return pl.ds(b * rows, rows) if isinstance(b, int) else tile_of(b, rows)


def own_kernel(blocks_of, x, wk_a, wk_b, wv, wq, k, v, q):
    blocks = blocks_of()
    rows = q.shape[0] // len(blocks)
    half = wk_a.shape[1]

    def key_step(j, carry):
        lanes = tile_of(j, TILE)
        k[:, lanes] = dot(x[...], wk_a[:, lanes]).astype(BF16)
        k[:, tile_of(j + half // TILE, TILE)] = dot(x[...], wk_b[:, lanes]).astype(BF16)
        return carry

    lax.fori_loop(0, half // TILE, key_step, 0)

    def step(j, carry):
        lanes = tile_of(j, TILE)
        v[:, lanes] = dot(x[...], wv[:, lanes]).astype(BF16)
        for n, b in enumerate(blocks):
            term = dot(x[block_rows(b, rows), :], wq[:, lanes])
            q[pl.ds(n * rows, rows), lanes] = term.astype(BF16)
        return carry

    lax.fori_loop(0, k.shape[1] // TILE, step, 0)


def own_projections(blocks_of, count, rows, x, wk_a, wk_b, wv, wq):
    total, depth = x.shape
    width = wv.shape[1]
    return pl.pallas_call(
        functools.partial(own_kernel, blocks_of),
        out_shape=[
            jax.ShapeDtypeStruct((r, width), BF16) for r in (total, total, count * rows)
        ],
        in_specs=[pl.BlockSpec(memory_space=VMEM)] * 5,
        out_specs=[pl.BlockSpec(memory_space=VMEM)] * 3,
        compiler_params=params(4),
        cost_estimate=cost(2 * total + count * rows, depth, width),
    )(x, wk_a, wk_b, wv, wq)


def queries_kernel(blocks_of, x, wq, q):
    blocks = blocks_of()
    rows = q.shape[0] // len(blocks)

    def step(j, carry):
        lanes = tile_of(j, TILE)
        for n, b in enumerate(blocks):
            term = dot(x[block_rows(b, rows), :], wq[:, lanes])
            q[pl.ds(n * rows, rows), lanes] = term.astype(BF16)
        return carry

    lax.fori_loop(0, q.shape[1] // TILE, step, 0)


def more_queries(blocks_of, count, rows, x, wq):
    depth, width = wq.shape
    return pl.pallas_call(
        functools.partial(queries_kernel, blocks_of),
        out_shape=jax.ShapeDtypeStruct((count * rows, width), BF16),
        in_specs=[pl.BlockSpec(memory_space=VMEM)] * 2,
        out_specs=pl.BlockSpec(memory_space=VMEM),
        compiler_params=params(4),
        cost_estimate=cost(count * rows, depth, width),
    )(x, wq)


def weigh_kernel(first, blocks_of, lens, q, km_a, km_b, ko, p, bias):
    blocks = blocks_of()
    width = q.shape[1]
    keys = ko.shape[0]
    rows = p.shape[1] // len(blocks)
    group = lax.axis_index("seq")
    total = lens.shape[0]
    own_len = lens[group]
    mem_len = lens[lax.rem(group + total - 1, total)]
    scale = math.log2(math.e) / math.sqrt(HEAD_DIM)
    nt = (((1,), (1,)), ((), ()))
    mem_cols, own_cols = pl.ds(0, keys), pl.ds(keys, keys)
    split = km_a.shape[1] // HEAD_DIM
    col = lax.broadcasted_iota(jnp.int32, (rows, keys), 1)
    bias[:, mem_cols] = jnp.where(col < mem_len, 0.0, -1e30)

    for n, b in enumerate(blocks):
        here = pl.ds(n * rows, rows)
        row = lax.broadcasted_iota(jnp.int32, (rows, keys), 0) + b * rows
        bias[:, own_cols] = jnp.where((col <= row) & (col < own_len), 0.0, -1e30)
        for h in range(width // HEAD_DIM):
            lanes = pl.ds(h * HEAD_DIM, HEAD_DIM)
            one = q[pl.ds((first + n) * rows, rows), lanes]
            km, at = (km_a, h) if h < split else (km_b, h - split)
            mem_lanes = pl.ds(at * HEAD_DIM, HEAD_DIM)
            sm = lax.dot_general(one, km[:, mem_lanes], nt, preferred_element_type=F32)
            so = lax.dot_general(one, ko[:, lanes], nt, preferred_element_type=F32)
            sm = sm + bias[:, mem_cols]
            so = so + bias[:, own_cols]
            top = jnp.maximum(
                jnp.max(sm, axis=-1, keepdims=True), jnp.max(so, axis=-1, keepdims=True)
            )
            pm = jnp.exp2((sm - top) * scale)
            po = jnp.exp2((so - top) * scale)
            norm = jnp.sum(pm, axis=-1, keepdims=True) + jnp.sum(po, axis=-1, keepdims=True)
            inverse = 1.0 / norm
            p[h, here, mem_cols] = (pm * inverse).astype(BF16)
            p[h, here, own_cols] = (po * inverse).astype(BF16)


def weigh(first, blocks_of, count, rows, lens, q, km_a, km_b, ko):
    width = q.shape[1]
    keys = ko.shape[0]
    heads = width // HEAD_DIM
    return pl.pallas_call(
        functools.partial(weigh_kernel, first, blocks_of),
        out_shape=jax.ShapeDtypeStruct((heads, count * rows, 2 * keys), BF16),
        in_specs=[pl.BlockSpec(memory_space=pltpu.SMEM)] + [pl.BlockSpec(memory_space=VMEM)] * 4,
        out_specs=pl.BlockSpec(memory_space=VMEM),
        scratch_shapes=[VMEM((rows, 2 * keys), F32)],
        compiler_params=params(4),
        cost_estimate=pl.CostEstimate(
            flops=4 * count * rows * width * keys,
            bytes_accessed=0,
            transcendentals=heads * count * rows * 2 * keys,
        ),
    )(lens, q, km_a, km_b, ko)


def context(p, vm, vo, ctx):
    keys, width = vo.shape
    for h in range(width // HEAD_DIM):
        lanes = pl.ds(h * HEAD_DIM, HEAD_DIM)
        mixed = dot(p[h, :, pl.ds(0, keys)], vm[:, lanes])
        mixed = mixed + dot(p[h, :, pl.ds(keys, keys)], vo[:, lanes])
        ctx[:, lanes] = mixed.astype(BF16)


def column_tiles(cols):
    wide = 2 * TILE
    return [(j, min(wide, cols - j)) for j in range(0, cols, wide)]


def attend_kernel(split, p, vm, vo, wo, *refs):
    outs, ctx = refs[:-1], refs[-1]
    context(p, vm, vo, ctx)
    rows = outs[0].shape[0]
    for out, (block, start, size) in zip(outs, split):
        for first, width in column_tiles(size):
            here = pl.ds(block * rows, rows)
            term = dot(ctx[here, :], wo[:, pl.ds(start + first, width)])
            out[:, pl.ds(first, width)] = term.astype(out.dtype)


def attend(count, split, kinds, rows, p, vm, vo, wo):
    keys, width = vo.shape
    depth = wo.shape[1]
    return pl.pallas_call(
        functools.partial(attend_kernel, split),
        out_shape=[
            jax.ShapeDtypeStruct((rows, cols), kind) for (_, _, cols), kind in zip(split, kinds)
        ],
        in_specs=[pl.BlockSpec(memory_space=VMEM)] * 4,
        out_specs=[pl.BlockSpec(memory_space=VMEM)] * len(split),
        scratch_shapes=[VMEM((count * rows, width), BF16)],
        compiler_params=params(4),
        cost_estimate=pl.CostEstimate(
            flops=2 * count * rows * width * (depth + 2 * keys),
            bytes_accessed=2 * depth * width,
            transcendentals=0,
        ),
    )(p, vm, vo, wo)


def direct_kernel(start, p, vm, vo, wo, out, ctx):
    context(p, vm, vo, ctx)
    for first, width in column_tiles(out.shape[1]):
        term = dot(ctx[...], wo[:, pl.ds(start + first, width)])
        out[:, pl.ds(first, width)] = term.astype(BF16)


def direct(start, cols, p, vm, vo, wo):
    keys, width = vo.shape
    rows = p.shape[1]
    return pl.pallas_call(
        functools.partial(direct_kernel, start),
        out_shape=[jax.ShapeDtypeStruct((rows, c), BF16) for c in (cols, width)],
        in_specs=[pl.BlockSpec(memory_space=VMEM)] * 4,
        out_specs=[pl.BlockSpec(memory_space=VMEM)] * 2,
        compiler_params=params(4),
        cost_estimate=pl.CostEstimate(
            flops=2 * rows * width * (cols + 2 * keys),
            bytes_accessed=2 * cols * width,
            transcendentals=0,
        ),
    )(p, vm, vo, wo)


def joined_kernel(start, ctx, wo, got, out):
    for first, width in column_tiles(out.shape[1]):
        here = pl.ds(first, width)
        term = dot(ctx[...], wo[:, pl.ds(start + first, width)])
        out[:, here] = (term + got[:, here].astype(F32)).astype(BF16)


def joined(start, ctx, wo, got):
    rows, width = ctx.shape
    return pl.pallas_call(
        functools.partial(joined_kernel, start),
        out_shape=jax.ShapeDtypeStruct(got.shape, BF16),
        in_specs=[pl.BlockSpec(memory_space=VMEM)] * 3,
        out_specs=pl.BlockSpec(memory_space=VMEM),
        compiler_params=params(4),
        cost_estimate=cost(rows, width, got.shape[1]),
    )(ctx, wo, got)


def to_next(x):
    devices = lax.axis_size("seq")
    return lax.ppermute(x, "seq", [(i, (i + 1) % devices) for i in range(devices)])


def swapped(x, bit):
    return lax.ppermute(x, "tp", [(i, i ^ bit) for i in range(lax.axis_size("tp"))])


def final_kernel(own, xa, xb, ya, yb, out_hbm, out, sems):
    rows, cut = xa.shape
    left, right = pl.ds(0, cut), pl.ds(cut, own.shape[1] - cut)
    part = rows // sems.shape[0]
    copies = []
    for k in range(sems.shape[0]):
        here = pl.ds(k * part, part)
        low = own[here, left] + xa[here, :].astype(F32) + ya[here, :].astype(F32)
        high = own[here, right] + xb[here, :].astype(F32) + yb[here, :].astype(F32)
        out[here, left] = low.astype(BF16)
        out[here, right] = high.astype(BF16)
        copy = pltpu.make_async_copy(out.at[here, :], out_hbm.at[0, here, :], sems.at[k])
        copy.start()
        copies.append(copy)
    for copy in copies:
        copy.wait()


def final(own, *parts):
    return pl.pallas_call(
        final_kernel,
        out_shape=jax.ShapeDtypeStruct((1, *own.shape), BF16),
        in_specs=[pl.BlockSpec(memory_space=VMEM)] * 5,
        out_specs=pl.BlockSpec(memory_space=pltpu.HBM),
        scratch_shapes=[VMEM(own.shape, BF16), pltpu.SemaphoreType.DMA((4,))],
        compiler_params=params(4),
        cost_estimate=pl.CostEstimate(
            flops=3 * own.size, bytes_accessed=14 * own.size, transcendentals=0
        ),
    )(own, *parts)


def body(layer_input, memory, lens, wq, wk, wv, wo):
    x = layer_input[0]
    shares = lax.axis_size("tp")
    rows = x.shape[0] // shares
    depth = wo.shape[1]
    cut = depth // 2 + HEAD_DIM
    whole, lower, upper = (0, depth), (0, cut), (cut, depth - cut)

    def block(bits):
        return lambda: [lax.axis_index("tp") ^ b for b in bits]

    part = wk.shape[1] // 2
    sent_a, wk_a, near_memory = streamed(memory[0], wk, 0, part, True)
    mem_keys_a = to_next(sent_a)
    sent_b, wk_b = streamed(near_memory, wk, part, part, False)
    mem_keys_b = to_next(sent_b)
    (sent_values,) = resident(near_memory, wv)
    mem_values = to_next(sent_values)
    weights = (wk_a, wk_b, wv, wq)
    if shares != 4:
        every = (lambda: list(range(shares)), shares, rows)
        own_keys, own_values, queries = own_projections(*every, x, *weights)
        p = weigh(0, *every, lens, queries, mem_keys_a, mem_keys_b, own_keys)
        split = tuple((b, *whole) for b in range(shares))
        terms = attend(shares, split, (F32,) * shares, rows, p, mem_values, own_values, wo)
        summed = lax.psum_scatter(
            jnp.concatenate(terms), "tp", scatter_dimension=0, tiled=True
        )
        return summed.astype(BF16)[None]

    own_keys, own_values, q_far = own_projections(block([3]), 1, rows, x, *weights)
    sides = (mem_keys_a, mem_keys_b, own_keys)
    tail = (mem_values, own_values, wo)
    p_far = weigh(0, block([3]), 1, rows, lens, q_far, *sides)
    far_a, far_b = attend(1, ((0, *lower), (0, *upper)), (BF16, BF16), rows, p_far, *tail)
    got_a = swapped(far_a, 1)
    got_b = swapped(far_b, 2)
    q_near = more_queries(block([1, 2]), 2, rows, x, wq)
    p_side = weigh(0, block([1]), 1, rows, lens, q_near, *sides)
    xa, side_ctx = direct(*lower, p_side, *tail)
    from_xa = swapped(xa, 1)
    q_near, side_ctx = lax.optimization_barrier((q_near, side_ctx))
    p_below = weigh(1, block([2]), 1, rows, lens, q_near, *sides)
    yb, below_ctx = direct(*upper, p_below, *tail)
    from_yb = swapped(yb, 2)
    xb = joined(cut, side_ctx, wo, got_b)
    ya = joined(0, below_ctx, wo, got_a)
    from_xb, from_ya = swapped(xb, 1), swapped(ya, 2)
    x, below_ctx = lax.optimization_barrier((x, below_ctx))
    q_mine = more_queries(block([0]), 1, rows, x, wq)
    p_mine = weigh(0, block([0]), 1, rows, lens, q_mine, *sides)
    (own,) = attend(1, ((0, *whole),), (F32,), rows, p_mine, *tail)
    return final(own, from_xa, from_xb, from_ya, from_yb)


def solution(mesh):
    return jax.shard_map(
        body,
        mesh=mesh,
        in_specs=(
            P("seq", None, None),
            P("seq", None, None),
            P(),
            P(None, "tp"),
            P(None, "tp"),
            P(None, "tp"),
            P("tp", None),
        ),
        out_specs=P("seq", "tp", None),
        check_vma=False,
    )
```

time: 81.6 us -> 76.1 us (0.933)
  waiting for transfers between devices: 26.1 us -> 15 us
  Pallas kernels: 43.7 us -> 47 us
  starting transfers between devices: 11 us -> 12.4 us
    pallas_call x8 -> x15, Pallas kernels: 21.6 us -> 40.7 us  [the longest x1 11 us: own_projections(): pl.pallas_call(functools.partial(own_kernel, blocks_of), out_shape=[jax.S...]
    pallas_call x2 -> x1, Pallas kernels: 20.8 us -> 5.17 us  [resident(): pl.pallas_call(functools.partial(resident_kernel, count), out_shape=[jax....]
    ppermute x6, waiting for transfers between devices: 16.8 us -> 10.5 us  [swapped(): lax.ppermute(x, 'tp', [(i, i ^ bit) for i in range(lax.axis_size('tp'))])]
    ppermute x2 -> x3, waiting for transfers between devices: 9.34 us -> 4.48 us  [to_next(): lax.ppermute(x, 'seq', [(i, (i + 1) % devices) for i in range(devices)])]
    ppermute x2 -> x3, starting transfers between devices: 3.22 us -> 3.82 us  [to_next(): lax.ppermute(x, 'seq', [(i, (i + 1) % devices) for i in range(devices)])]
  transfers between devices with their start and end apart: 8 -> 9, of which waited for: 4 -> 3; matrix products, arithmetic and copies ran while one was open for 0% -> 0% of each run, Pallas kernels for 35% -> 52%
where the time goes in v3:
time: 76.1 us; the launch traced here: 75.9 us
  Pallas kernels  47 us (62%)
  waiting for transfers between devices  15 us (20%)
  starting transfers between devices  12.4 us (16%)
  local copies, waits for them, and re-layouts  1.16 us (2%)
    pallas_call x1, Pallas kernels, own_projections(): pl.pallas_call(functools.partial(own_kernel, blocks_of), out_shape=[jax.S...  11 us
    ppermute x6, waiting for transfers between devices, swapped(): lax.ppermute(x, 'tp', [(i, i ^ bit) for i in range(lax.axis_size('tp'))])  10.5 us
    ppermute x6, starting transfers between devices, swapped(): lax.ppermute(x, 'tp', [(i, i ^ bit) for i in range(lax.axis_size('tp'))])  8.58 us
    pallas_call x4, Pallas kernels, weigh(): pl.pallas_call(functools.partial(weigh_kernel, first, blocks_of), out_sha...  8.53 us
    pallas_call x2, Pallas kernels, streamed(): pl.pallas_call(functools.partial(streamed_kernel, start), out_shape=[jax....  8.01 us
    pallas_call x1, Pallas kernels, resident(): pl.pallas_call(functools.partial(resident_kernel, count), out_shape=[jax....  5.17 us
    pallas_call x2, Pallas kernels, more_queries(): pl.pallas_call(functools.partial(queries_kernel, blocks_of), out_shape=ja...  5.14 us
    ppermute x3, waiting for transfers between devices, to_next(): lax.ppermute(x, 'seq', [(i, (i + 1) % devices) for i in range(devices)])  4.48 us
  transfers between devices with their start and end apart: 9, of which 3 were waited for; matrix products, arithmetic and copies ran while one was open for 0% of the time, Pallas kernels for 52%

profile of v3, /device:TPU:0, one launch (start us, length us, event | category | flops | bytes accessed | tf_op | source)
XLA Modules:
  0.0 75.9 jit_solution(8075689579690445464)
XLA Ops:
  0.0 0.0 copy-start.2
  0.0 0.0 slice-start.2
  0.0 4.2 %shard_map.74 = (bf16[512,512]{1,0:T(8,128)(2,1)S(1)}, bf16[4096,512]{1,0:T(8,128)(2,1)S(1)}, bf16[512,4096]{1,0:T(8,128)(2,1)S(1)}) custom-call(bf16[512,4096]{1,0:T(8,128)(2,1)} %bitcast.9, bf16[4096,1024]{1,0:T(8,128)(2,1)} %w_hbm.3), custom_call_target="tpu_custom_call" | custom-call | flops 2147483648 | bytes 8912896 | tf_op jit(solution)/shard_map/pallas_call | solution.py:77
  4.2 0.5 collective-permute-start
  4.8 1.1 %copy-done.2 = bf16[4096,1024]{1,0:T(8,128)(2,1)S(1)} copy-done((bf16[4096,1024]{1,0:T(8,128)(2,1)S(1)}, bf16[4096,1024]{1,0:T(8,128)(2,1)}, u32[]{:S(2)}) %copy-start.2) | copy-done | bytes 8388632
  5.9 0.0 slice-start.3
  5.9 5.2 %shard_map.78 = bf16[512,1024]{1,0:T(8,128)(2,1)S(1)} custom-call(bf16[512,4096]{1,0:T(8,128)(2,1)S(1)} %get-tuple-element.23.x_hbm.x, bf16[4096,1024]{1,0:T(8,128)(2,1)S(1)} %copy-done.2), custom_call_target="tpu_custom_call" | custom-call | flops 4294967296 | bytes 13631488 | tf_op jit(solution)/shard_map/pallas_call | solution.py:106
  11.1 0.0 copy-start
  11.1 1.6 %collective-permute-start.2 = (bf16[512,1024]{1,0:T(8,128)(2,1)S(1)}, bf16[512,1024]{1,0:T(8,128)(2,1)S(1)}, u32[]{:S(2)}, u32[]{:S(2)}) collective-permute-start(bf16[512,1024]{1,0:T(8,128)(2,1)S(1)} %shard_map.78), channel_id=1, source_target_pairs={{0,4},{4,8},{8,12},{12,16},{16,20},{20,24},{24,28},{28,0},{1,5},{5... | collective-permute-start | bytes 3145736 | tf_op jit(solution)/shard_map/ppermute | solution.py:335
  12.7 3.8 %shard_map.75 = (bf16[512,512]{1,0:T(8,128)(2,1)S(1)}, bf16[4096,512]{1,0:T(8,128)(2,1)S(1)}) custom-call(bf16[512,4096]{1,0:T(8,128)(2,1)S(1)} %get-tuple-element.23.x_hbm.x, bf16[4096,1024]{1,0:T(8,128)(2,1)} %w_hbm.3), custom_call_target="tpu_custom_call" | custom-call | flops 2147483648 | bytes 8912896 | tf_op jit(solution)/shard_map/pallas_call | solution.py:77
  16.5 1.7 %collective-permute-start.1 = (bf16[512,512]{1,0:T(8,128)(2,1)S(1)}, bf16[512,512]{1,0:T(8,128)(2,1)S(1)}, u32[]{:S(2)}, u32[]{:S(2)}) collective-permute-start(bf16[512,512]{1,0:T(8,128)(2,1)S(1)} %get-tuple-element.24), channel_id=1, source_target_pairs={{0,4},{4,8},{8,12},{12,16},{16,20},{20,24},{24,28},{28,0},{1,5},{5... | collective-permute-start | bytes 1572872 | tf_op jit(solution)/shard_map/ppermute | solution.py:335
  18.2 0.0 slice-start
  18.2 0.0 slice-done.2
  18.2 0.0 slice-done.3
  18.2 0.0 copy-done
  18.2 0.0 copy-start.1
  18.2 0.0 slice-start.1
  18.2 11.0 %shard_map.76 = (bf16[512,1024]{1,0:T(8,128)(2,1)S(1)}, bf16[512,1024]{1,0:T(8,128)(2,1)S(1)}, bf16[128,1024]{1,0:T(8,128)(2,1)S(1)}) custom-call(bf16[512,4096]{1,0:T(8,128)(2,1)S(1)} %bitcast.6, bf16[4096,512]{1,0:T(8,128)(2,1)S(1)} %get-tuple-element.25.wk_a, bf16[4096,512]{1,0:T(8,128)(2,1)S(1)} %get-tuple-element.26.wk_b, ...), custom_call_target="tpu_custom_call" | custom-call | flops 9663676416 | bytes 20185088 | tf_op jit(solution)/shard_map/pallas_call | solution.py:148
  29.3 0.0 collective-permute-done.km_a
  29.3 4.5 %collective-permute-done.1.km_b = bf16[512,512]{1,0:T(8,128)(2,1)S(1)} collective-permute-done((bf16[512,512]{1,0:T(8,128)(2,1)S(1)}, bf16[512,512]{1,0:T(8,128)(2,1)S(1)}, u32[]{:S(2)}, u32[]{:S(2)}) %collective-permute-start.1) | collective-permute-done | bytes 524320 | tf_op jit(solution)/shard_map/ppermute | solution.py:335
  33.7 0.0 copy-done.1
  33.7 2.1 %shard_map.85.p = bf16[8,128,1024]{2,1,0:T(8,128)(2,1)S(1)} custom-call(s32[8]{0:T(128)S(1)} %copy-done.1, bf16[128,1024]{1,0:T(8,128)(2,1)S(1)} %get-tuple-element.35.q, bf16[512,512]{1,0:T(8,128)(2,1)S(1)} %collective-permute-done.km_a, bf16[512,512]{1,0:T(8,128)(2,1)S(1)} %collective-permute-done.1.km_b, bf16[512,1024]{1,0:T(8,128)(2,1)S(1)} %get-tuple-element.27.ko), custom_call_target="tpu_custom_call" | custom-call | flops 268435456 | tf_op jit(solution)/shard_map/pallas_call | solution.py:230
  35.9 0.0 collective-permute-done.2.vm
  35.9 0.0 slice-done
  35.9 0.0 slice-done.1
  35.9 1.9 %shard_map.86 = (bf16[128,2176]{1,0:T(8,128)(2,1)S(1)}, bf16[128,1920]{1,0:T(8,128)(2,1)S(1)}) custom-call(bf16[8,128,1024]{2,1,0:T(8,128)(2,1)S(1)} %shard_map.85.p, bf16[512,1024]{1,0:T(8,128)(2,1)S(1)} %collective-permute-done.2.vm, bf16[512,1024]{1,0:T(8,128)(2,1)S(1)} %get-tuple-element.28.vo, bf16[1024,4096]{1,0:T(8,128)(2,1)S(1)} %bitcast.3), custom_call_target="tpu_custom_call" | custom-call | flops 1342177280 | bytes 8388608 | tf_op jit(solution)/shard_map/pallas_call | solution.py:273
  37.8 2.1 %collective-permute-start.6 = (bf16[128,2176]{1,0:T(8,128)(2,1)S(1)}, bf16[128,2176]{1,0:T(8,128)(2,1)S(1)}, u32[]{:S(2)}, u32[]{:S(2)}) collective-permute-start(bf16[128,2176]{1,0:T(8,128)(2,1)S(1)} %get-tuple-element.37), channel_id=1, source_target_pairs={{0,1},{1,0},{2,3},{3,2},{4,5},{5,4},{6,7},{7,6},{8,9},{9,8},{10,11... | collective-permute-start | bytes 1671176 | tf_op jit(solution)/shard_map/ppermute | solution.py:339
  39.9 1.5 %collective-permute-start.4 = (bf16[128,1920]{1,0:T(8,128)(2,1)S(1)}, bf16[128,1920]{1,0:T(8,128)(2,1)S(1)}, u32[]{:S(2)}, u32[]{:S(2)}) collective-permute-start(bf16[128,1920]{1,0:T(8,128)(2,1)S(1)} %get-tuple-element.36), channel_id=1, source_target_pairs={{0,2},{1,3},{2,0},{3,1},{4,6},{5,7},{6,4},{7,5},{8,10},{9,11},{10,... | collective-permute-start | bytes 1474568 | tf_op jit(solution)/shard_map/ppermute | solution.py:339
  41.4 3.1 %shard_map.73.q = bf16[256,1024]{1,0:T(8,128)(2,1)S(1)} custom-call(bf16[512,4096]{1,0:T(8,128)(2,1)S(1)} %bitcast.7, bf16[4096,1024]{1,0:T(8,128)(2,1)S(1)} %bitcast.5), custom_call_target="tpu_custom_call" | custom-call | flops 2147483648 | bytes 11010048 | tf_op jit(solution)/shard_map/pallas_call | solution.py:176
  44.5 2.1 %shard_map.77.p = bf16[8,128,1024]{2,1,0:T(8,128)(2,1)S(1)} custom-call(s32[8]{0:T(128)S(1)} %copy-done.1, bf16[256,1024]{1,0:T(8,128)(2,1)S(1)} %shard_map.73.q, bf16[512,512]{1,0:T(8,128)(2,1)S(1)} %collective-permute-done.km_a, bf16[512,512]{1,0:T(8,128)(2,1)S(1)} %collective-permute-done.1.km_b, bf16[512,1024]{1,0:T(8,128)(2,1)S(1)} %get-tuple-element.27.ko), custom_call_target="tpu_custom_call" | custom-call | flops 268435456 | tf_op jit(solution)/shard_map/pallas_call | solution.py:230
  46.7 1.4 %shard_map.79 = (bf16[128,2176]{1,0:T(8,128)(2,1)S(1)}, bf16[128,1024]{1,0:T(8,128)(2,1)S(1)}) custom-call(bf16[8,128,1024]{2,1,0:T(8,128)(2,1)S(1)} %shard_map.77.p, bf16[512,1024]{1,0:T(8,128)(2,1)S(1)} %collective-permute-done.2.vm, bf16[512,1024]{1,0:T(8,128)(2,1)S(1)} %get-tuple-element.28.vo, bf16[1024,4096]{1,0:T(8,128)(2,1)S(1)} %bitcast.3), custom_call_target="tpu_custom_call" | custom-call | flops 838860800 | bytes 4456448 | tf_op jit(solution)/shard_map/pallas_call | solution.py:300
  48.1 0.6 collective-permute-start.3
  48.7 2.1 %shard_map.80.p = bf16[8,128,1024]{2,1,0:T(8,128)(2,1)S(1)} custom-call(s32[8]{0:T(128)S(1)} %copy-done.1, bf16[256,1024]{1,0:T(8,128)(2,1)S(1)} %shard_map.73.q, bf16[512,512]{1,0:T(8,128)(2,1)S(1)} %collective-permute-done.km_a, bf16[512,512]{1,0:T(8,128)(2,1)S(1)} %collective-permute-done.1.km_b, bf16[512,1024]{1,0:T(8,128)(2,1)S(1)} %get-tuple-element.27.ko), custom_call_target="tpu_custom_call" | custom-call | flops 268435456 | tf_op jit(solution)/shard_map/pallas_call | solution.py:230
  50.8 1.3 %shard_map.81 = (bf16[128,1920]{1,0:T(8,128)(2,1)S(1)}, bf16[128,1024]{1,0:T(8,128)(2,1)S(1)}) custom-call(bf16[8,128,1024]{2,1,0:T(8,128)(2,1)S(1)} %shard_map.80.p, bf16[512,1024]{1,0:T(8,128)(2,1)S(1)} %collective-permute-done.2.vm, bf16[512,1024]{1,0:T(8,128)(2,1)S(1)} %get-tuple-element.28.vo, bf16[1024,4096]{1,0:T(8,128)(2,1)S(1)} %bitcast.3), custom_call_target="tpu_custom_call" | custom-call | flops 771751936 | bytes 3932160 | tf_op jit(solution)/shard_map/pallas_call | solution.py:300
  52.1 1.0 %collective-permute-done.6.got = bf16[128,2176]{1,0:T(8,128)(2,1)S(1)} collective-permute-done((bf16[128,2176]{1,0:T(8,128)(2,1)S(1)}, bf16[128,2176]{1,0:T(8,128)(2,1)S(1)}, u32[]{:S(2)}, u32[]{:S(2)}) %collective-permute-start.6) | collective-permute-done | bytes 557088 | tf_op jit(solution)/shard_map/ppermute | solution.py:339
  53.2 0.8 %shard_map.88 = bf16[128,2176]{1,0:T(8,128)(2,1)S(1)} custom-call(bf16[128,1024]{1,0:T(8,128)(2,1)S(1)} %get-tuple-element.31.ctx, bf16[1024,4096]{1,0:T(8,128)(2,1)S(1)} %bitcast.3, bf16[128,2176]{1,0:T(8,128)(2,1)S(1)} %collective-permute-done.6.got), custom_call_target="tpu_custom_call" | custom-call | flops 570425344 | bytes 5275648 | tf_op jit(solution)/shard_map/pallas_call | solution.py:323
  54.0 2.3 %collective-permute-start.7 = (bf16[128,2176]{1,0:T(8,128)(2,1)S(1)}, bf16[128,2176]{1,0:T(8,128)(2,1)S(1)}, u32[]{:S(2)}, u32[]{:S(2)}) collective-permute-start(bf16[128,2176]{1,0:T(8,128)(2,1)S(1)} %shard_map.88), channel_id=1, source_target_pairs={{0,2},{1,3},{2,0},{3,1},{4,6},{5,7},{6,4},{7,5},{8,10},{9,11},{10,... | collective-permute-start | bytes 1671176 | tf_op jit(solution)/shard_map/ppermute | solution.py:339
  56.3 0.1 collective-permute-start.8
  56.4 0.0 collective-permute-done.4.got
  56.4 0.7 shard_map.87
  57.1 2.0 %collective-permute-start.5 = (bf16[128,1920]{1,0:T(8,128)(2,1)S(1)}, bf16[128,1920]{1,0:T(8,128)(2,1)S(1)}, u32[]{:S(2)}, u32[]{:S(2)}) collective-permute-start(bf16[128,1920]{1,0:T(8,128)(2,1)S(1)} %shard_map.87), channel_id=1, source_target_pairs={{0,1},{1,0},{2,3},{3,2},{4,5},{5,4},{6,7},{7,6},{8,9},{9,8},{10,11... | collective-permute-start | bytes 1474568 | tf_op jit(solution)/shard_map/ppermute | solution.py:339
  59.1 2.0 %shard_map.82.q = bf16[128,1024]{1,0:T(8,128)(2,1)S(1)} custom-call(bf16[512,4096]{1,0:T(8,128)(2,1)S(1)} %bitcast.8, bf16[4096,1024]{1,0:T(8,128)(2,1)S(1)} %bitcast.5), custom_call_target="tpu_custom_call" | custom-call | flops 1073741824 | bytes 9699328 | tf_op jit(solution)/shard_map/pallas_call | solution.py:176
  61.2 2.1 %shard_map.83.p = bf16[8,128,1024]{2,1,0:T(8,128)(2,1)S(1)} custom-call(s32[8]{0:T(128)S(1)} %copy-done.1, bf16[128,1024]{1,0:T(8,128)(2,1)S(1)} %shard_map.82.q, bf16[512,512]{1,0:T(8,128)(2,1)S(1)} %collective-permute-done.km_a, bf16[512,512]{1,0:T(8,128)(2,1)S(1)} %collective-permute-done.1.km_b, bf16[512,1024]{1,0:T(8,128)(2,1)S(1)} %get-tuple-element.27.ko), custom_call_target="tpu_custom_call" | custom-call | flops 268435456 | tf_op jit(solution)/shard_map/pallas_call | solution.py:230
  63.3 1.9 %shard_map.84.own = f32[128,4096]{1,0:T(8,128)S(1)} custom-call(bf16[8,128,1024]{2,1,0:T(8,128)(2,1)S(1)} %shard_map.83.p, bf16[512,1024]{1,0:T(8,128)(2,1)S(1)} %collective-permute-done.2.vm, bf16[512,1024]{1,0:T(8,128)(2,1)S(1)} %get-tuple-element.28.vo, bf16[1024,4096]{1,0:T(8,128)(2,1)S(1)} %bitcast.3), custom_call_target="tpu_custom_call" | custom-call | flops 1342177280 | bytes 8388608 | tf_op jit(solution)/shard_map/pallas_call | solution.py:273
  65.2 9.5 %collective-permute-done.8.yb = bf16[128,1920]{1,0:T(8,128)(2,1)S(1)} collective-permute-done((bf16[128,1920]{1,0:T(8,128)(2,1)S(1)}, bf16[128,1920]{1,0:T(8,128)(2,1)S(1)}, u32[]{:S(2)}, u32[]{:S(2)}) %collective-permute-start.8) | collective-permute-done | bytes 491552 | tf_op jit(solution)/shard_map/ppermute | solution.py:339
  74.7 0.0 collective-permute-done.3.xa
  74.7 0.0 collective-permute-done.5.xb
  74.7 0.0 collective-permute-done.7.ya
  74.7 1.1 %shard_map.89 = bf16[1,128,4096]{2,1,0:T(8,128)(2,1)} custom-call(f32[128,4096]{1,0:T(8,128)S(1)} %shard_map.84.own, bf16[128,2176]{1,0:T(8,128)(2,1)S(1)} %collective-permute-done.3.xa, bf16[128,1920]{1,0:T(8,128)(2,1)S(1)} %collective-permute-done.5.xb, bf16[128,2176]{1,0:T(8,128)(2,1)S(1)} %collective-permute-done.7.ya, ...), custom_call_target="tpu_custom_call" | custom-call | flops 1572864 | bytes 7340032 | tf_op jit(solution)/shard_map/pallas_call | solution.py:361
  (2 shorter events, 0.0 us)
Async XLA Ops:
  0.0 5.9 %copy-start.2 = (bf16[4096,1024]{1,0:T(8,128)(2,1)S(1)}, bf16[4096,1024]{1,0:T(8,128)(2,1)}, u32[]{:S(2)}) copy-start(bf16[4096,1024]{1,0:T(8,128)(2,1)} %refs_0_.1) | copy-start | bytes 25165828
  0.0 18.2 %slice-start.2 = ((s8[8388608]{0:T(1024)(128)(4,1)}), s8[4194304]{0:T(1024)(128)(4,1)S(1)}, s32[]{:S(2)}) async-start(s8[8388608]{0:T(1024)(128)(4,1)} %bitcast.4), calls=%async_computation.2 | async-start | bytes 8388608
  4.2 25.0 %collective-permute-start = (bf16[512,512]{1,0:T(8,128)(2,1)S(1)}, bf16[512,512]{1,0:T(8,128)(2,1)S(1)}, u32[]{:S(2)}, u32[]{:S(2)}) collective-permute-start(bf16[512,512]{1,0:T(8,128)(2,1)S(1)} %get-tuple-element.22), channel_id=1, source_target_pairs={{0,4},{4,8},{8,12},{12,16},{16,20},{20,24},{24,28},{28,0},{1,5},{5... | collective-permute-start | bytes 1572872 | tf_op jit(solution)/shard_map/ppermute | solution.py:335
  5.9 12.3 %slice-start.3 = ((s8[8388608]{0:T(1024)(128)(4,1)}), s8[4194304]{0:T(1024)(128)(4,1)S(1)}, s32[]{:S(2)}) async-start(s8[8388608]{0:T(1024)(128)(4,1)} %bitcast.4), calls=%async_computation.3 | async-start | bytes 8388608
  11.1 7.1 %copy-start = (bf16[1,512,4096]{2,1,0:T(8,128)(2,1)S(1)}, bf16[1,512,4096]{2,1,0:T(8,128)(2,1)}, u32[]{:S(2)}) copy-start(bf16[1,512,4096]{2,1,0:T(8,128)(2,1)} %param.7) | copy-start | bytes 12582916
  11.1 24.8 %collective-permute-start.2 = (bf16[512,1024]{1,0:T(8,128)(2,1)S(1)}, bf16[512,1024]{1,0:T(8,128)(2,1)S(1)}, u32[]{:S(2)}, u32[]{:S(2)}) collective-permute-start(bf16[512,1024]{1,0:T(8,128)(2,1)S(1)} %shard_map.78), channel_id=1, source_target_pairs={{0,4},{4,8},{8,12},{12,16},{16,20},{20,24},{24,28},{28,0},{1,5},{5... | collective-permute-start | bytes 3145736 | tf_op jit(solution)/shard_map/ppermute | solution.py:335
  16.5 17.2 %collective-permute-start.1 = (bf16[512,512]{1,0:T(8,128)(2,1)S(1)}, bf16[512,512]{1,0:T(8,128)(2,1)S(1)}, u32[]{:S(2)}, u32[]{:S(2)}) collective-permute-start(bf16[512,512]{1,0:T(8,128)(2,1)S(1)} %get-tuple-element.24), channel_id=1, source_target_pairs={{0,4},{4,8},{8,12},{12,16},{16,20},{20,24},{24,28},{28,0},{1,5},{5... | collective-permute-start | bytes 1572872 | tf_op jit(solution)/shard_map/ppermute | solution.py:335
  18.2 17.7 %slice-start = ((s8[8388608]{0:T(1024)(128)(4,1)}), s8[4194304]{0:T(1024)(128)(4,1)S(1)}, s32[]{:S(2)}) async-start(s8[8388608]{0:T(1024)(128)(4,1)} %bitcast.2), calls=%async_computation | async-start | bytes 8388608
  18.2 15.5 %copy-start.1 = (s32[8]{0:T(128)S(1)}, s32[8]{0:T(128)}, u32[]{:S(2)}) copy-start(s32[8]{0:T(128)} %lens.7) | copy-start | bytes 100
  18.2 17.7 %slice-start.1 = ((s8[8388608]{0:T(1024)(128)(4,1)}), s8[4194304]{0:T(1024)(128)(4,1)S(1)}, s32[]{:S(2)}) async-start(s8[8388608]{0:T(1024)(128)(4,1)} %bitcast.2), calls=%async_computation.1 | async-start | bytes 8388608
  37.8 15.3 %collective-permute-start.6 = (bf16[128,2176]{1,0:T(8,128)(2,1)S(1)}, bf16[128,2176]{1,0:T(8,128)(2,1)S(1)}, u32[]{:S(2)}, u32[]{:S(2)}) collective-permute-start(bf16[128,2176]{1,0:T(8,128)(2,1)S(1)} %get-tuple-element.37), channel_id=1, source_target_pairs={{0,1},{1,0},{2,3},{3,2},{4,5},{5,4},{6,7},{7,6},{8,9},{9,8},{10,11... | collective-permute-start | bytes 1671176 | tf_op jit(solution)/shard_map/ppermute | solution.py:339
  39.9 16.5 %collective-permute-start.4 = (bf16[128,1920]{1,0:T(8,128)(2,1)S(1)}, bf16[128,1920]{1,0:T(8,128)(2,1)S(1)}, u32[]{:S(2)}, u32[]{:S(2)}) collective-permute-start(bf16[128,1920]{1,0:T(8,128)(2,1)S(1)} %get-tuple-element.36), channel_id=1, source_target_pairs={{0,2},{1,3},{2,0},{3,1},{4,6},{5,7},{6,4},{7,5},{8,10},{9,11},{10,... | collective-permute-start | bytes 1474568 | tf_op jit(solution)/shard_map/ppermute | solution.py:339
  48.1 26.6 %collective-permute-start.3 = (bf16[128,2176]{1,0:T(8,128)(2,1)S(1)}, bf16[128,2176]{1,0:T(8,128)(2,1)S(1)}, u32[]{:S(2)}, u32[]{:S(2)}) collective-permute-start(bf16[128,2176]{1,0:T(8,128)(2,1)S(1)} %get-tuple-element.33), channel_id=1, source_target_pairs={{0,1},{1,0},{2,3},{3,2},{4,5},{5,4},{6,7},{7,6},{8,9},{9,8},{10,11... | collective-permute-start | bytes 1671176 | tf_op jit(solution)/shard_map/ppermute | solution.py:339
  54.0 20.7 %collective-permute-start.7 = (bf16[128,2176]{1,0:T(8,128)(2,1)S(1)}, bf16[128,2176]{1,0:T(8,128)(2,1)S(1)}, u32[]{:S(2)}, u32[]{:S(2)}) collective-permute-start(bf16[128,2176]{1,0:T(8,128)(2,1)S(1)} %shard_map.88), channel_id=1, source_target_pairs={{0,2},{1,3},{2,0},{3,1},{4,6},{5,7},{6,4},{7,5},{8,10},{9,11},{10,... | collective-permute-start | bytes 1671176 | tf_op jit(solution)/shard_map/ppermute | solution.py:339
  56.3 18.4 %collective-permute-start.8 = (bf16[128,1920]{1,0:T(8,128)(2,1)S(1)}, bf16[128,1920]{1,0:T(8,128)(2,1)S(1)}, u32[]{:S(2)}, u32[]{:S(2)}) collective-permute-start(bf16[128,1920]{1,0:T(8,128)(2,1)S(1)} %get-tuple-element.38), channel_id=1, source_target_pairs={{0,2},{1,3},{2,0},{3,1},{4,6},{5,7},{6,4},{7,5},{8,10},{9,11},{10,... | collective-permute-start | bytes 1474568 | tf_op jit(solution)/shard_map/ppermute | solution.py:339
  57.1 17.6 %collective-permute-start.5 = (bf16[128,1920]{1,0:T(8,128)(2,1)S(1)}, bf16[128,1920]{1,0:T(8,128)(2,1)S(1)}, u32[]{:S(2)}, u32[]{:S(2)}) collective-permute-start(bf16[128,1920]{1,0:T(8,128)(2,1)S(1)} %shard_map.87), channel_id=1, source_target_pairs={{0,1},{1,0},{2,3},{3,2},{4,5},{5,4},{6,7},{7,6},{8,9},{9,8},{10,11... | collective-permute-start | bytes 1474568 | tf_op jit(solution)/shard_map/ppermute | solution.py:339

commit v4 on v3

--- a/solution.py
+++ b/solution.py
@@ -90,13 +90,14 @@
 
 def resident_kernel(count, x, *refs):
     cols = refs[0].shape[1]
+    wide = min(2 * TILE, cols)
     for w, out in zip(refs[:count], refs[count:]):
 
         def step(j, carry, w=w, out=out):
-            out[:, tile_of(j, TILE)] = dot(x[...], w[:, tile_of(j, TILE)]).astype(BF16)
+            out[:, tile_of(j, wide)] = dot(x[...], w[:, tile_of(j, wide)]).astype(BF16)
             return carry
 
-        lax.fori_loop(0, cols // TILE, step, 0)
+        lax.fori_loop(0, cols // wide, step, 0)
 
 
 def resident(x, *ws):
@@ -122,24 +123,19 @@
     blocks = blocks_of()
     rows = q.shape[0] // len(blocks)
     half = wk_a.shape[1]
-
-    def key_step(j, carry):
-        lanes = tile_of(j, TILE)
-        k[:, lanes] = dot(x[...], wk_a[:, lanes]).astype(BF16)
-        k[:, tile_of(j + half // TILE, TILE)] = dot(x[...], wk_b[:, lanes]).astype(BF16)
-        return carry
-
-    lax.fori_loop(0, half // TILE, key_step, 0)
+    k[:, pl.ds(0, half)] = dot(x[...], wk_a[...]).astype(BF16)
+    k[:, pl.ds(half, half)] = dot(x[...], wk_b[...]).astype(BF16)
+    wide = min(2 * TILE, wv.shape[1])
 
     def step(j, carry):
-        lanes = tile_of(j, TILE)
+        lanes = tile_of(j, wide)
         v[:, lanes] = dot(x[...], wv[:, lanes]).astype(BF16)
         for n, b in enumerate(blocks):
             term = dot(x[block_rows(b, rows), :], wq[:, lanes])
             q[pl.ds(n * rows, rows), lanes] = term.astype(BF16)
         return carry
 
-    lax.fori_loop(0, k.shape[1] // TILE, step, 0)
+    lax.fori_loop(0, k.shape[1] // wide, step, 0)
 
 
 def own_projections(blocks_of, count, rows, x, wk_a, wk_b, wv, wq):
@@ -160,15 +156,16 @@
 def queries_kernel(blocks_of, x, wq, q):
     blocks = blocks_of()
     rows = q.shape[0] // len(blocks)
+    wide = min(2 * TILE, q.shape[1])
 
     def step(j, carry):
-        lanes = tile_of(j, TILE)
+        lanes = tile_of(j, wide)
         for n, b in enumerate(blocks):
             term = dot(x[block_rows(b, rows), :], wq[:, lanes])
             q[pl.ds(n * rows, rows), lanes] = term.astype(BF16)
         return carry
 
-    lax.fori_loop(0, q.shape[1] // TILE, step, 0)
+    lax.fori_loop(0, q.shape[1] // wide, step, 0)
 
 
 def more_queries(blocks_of, count, rows, x, wq):
@@ -376,7 +373,7 @@
     shares = lax.axis_size("tp")
     rows = x.shape[0] // shares
     depth = wo.shape[1]
-    cut = depth // 2 + HEAD_DIM
+    cut = depth // 2 + 2 * HEAD_DIM
     whole, lower, upper = (0, depth), (0, cut), (cut, depth - cut)
 
     def block(bits):

time: 76.1 us -> 75.3 us (0.989)
  Pallas kernels: 47 us -> 44.9 us
  waiting for transfers between devices: 15 us -> 16.5 us
    ppermute x6, waiting for transfers between devices: 10.5 us -> 11.4 us  [swapped(): lax.ppermute(x, 'tp', [(i, i ^ bit) for i in range(lax.axis_size('tp'))])]
    pallas_call x2, Pallas kernels: 5.14 us -> 4.27 us  [more_queries(): pl.pallas_call(functools.partial(queries_kernel, blocks_of), out_shape=ja...]
  transfers between devices with their start and end apart: 9 -> 9, of which waited for: 3 -> 3; matrix products, arithmetic and copies ran while one was open for 0% -> 0% of each run, Pallas kernels for 52% -> 50%
where the time goes in v4:
time: 75.3 us; the launch traced here: 75.2 us
  Pallas kernels  44.9 us (60%)
  waiting for transfers between devices  16.5 us (22%)
  starting transfers between devices  12.3 us (16%)
  local copies, waits for them, and re-layouts  1.16 us (2%)
    ppermute x6, waiting for transfers between devices, swapped(): lax.ppermute(x, 'tp', [(i, i ^ bit) for i in range(lax.axis_size('tp'))])  11.4 us
    pallas_call x1, Pallas kernels, own_projections(): pl.pallas_call(functools.partial(own_kernel, blocks_of), out_shape=[jax.S...  10.3 us
    pallas_call x4, Pallas kernels, weigh(): pl.pallas_call(functools.partial(weigh_kernel, first, blocks_of), out_sha...  8.54 us
    ppermute x6, starting transfers between devices, swapped(): lax.ppermute(x, 'tp', [(i, i ^ bit) for i in range(lax.axis_size('tp'))])  8.26 us
    pallas_call x2, Pallas kernels, streamed(): pl.pallas_call(functools.partial(streamed_kernel, start), out_shape=[jax....  8.01 us
    ppermute x3, waiting for transfers between devices, to_next(): lax.ppermute(x, 'seq', [(i, (i + 1) % devices) for i in range(devices)])  5.07 us
    pallas_call x1, Pallas kernels, resident(): pl.pallas_call(functools.partial(resident_kernel, count), out_shape=[jax....  4.69 us
    pallas_call x2, Pallas kernels, more_queries(): pl.pallas_call(functools.partial(queries_kernel, blocks_of), out_shape=ja...  4.27 us
  transfers between devices with their start and end apart: 9, of which 3 were waited for; matrix products, arithmetic and copies ran while one was open for 0% of the time, Pallas kernels for 50%

profile of v4, /device:TPU:0, one launch (start us, length us, event | category | flops | bytes accessed | tf_op | source)
XLA Modules:
  0.0 75.2 jit_solution(11916089492065032291)
XLA Ops:
  0.0 0.0 copy-start.2
  0.0 0.0 slice-start.2
  0.0 4.2 %shard_map.74 = (bf16[512,512]{1,0:T(8,128)(2,1)S(1)}, bf16[4096,512]{1,0:T(8,128)(2,1)S(1)}, bf16[512,4096]{1,0:T(8,128)(2,1)S(1)}) custom-call(bf16[512,4096]{1,0:T(8,128)(2,1)} %bitcast.9, bf16[4096,1024]{1,0:T(8,128)(2,1)} %w_hbm.3), custom_call_target="tpu_custom_call" | custom-call | flops 2147483648 | bytes 8912896 | tf_op jit(solution)/shard_map/pallas_call | solution.py:77
  4.2 0.5 collective-permute-start
  4.8 1.1 %copy-done.2 = bf16[4096,1024]{1,0:T(8,128)(2,1)S(1)} copy-done((bf16[4096,1024]{1,0:T(8,128)(2,1)S(1)}, bf16[4096,1024]{1,0:T(8,128)(2,1)}, u32[]{:S(2)}) %copy-start.2) | copy-done | bytes 8388632
  5.9 0.0 slice-start.3
  5.9 4.7 %shard_map.78 = bf16[512,1024]{1,0:T(8,128)(2,1)S(1)} custom-call(bf16[512,4096]{1,0:T(8,128)(2,1)S(1)} %get-tuple-element.23.x_hbm.x, bf16[4096,1024]{1,0:T(8,128)(2,1)S(1)} %copy-done.2), custom_call_target="tpu_custom_call" | custom-call | flops 4294967296 | bytes 13631488 | tf_op jit(solution)/shard_map/pallas_call | solution.py:107
  10.6 0.0 copy-start
  10.6 1.6 %collective-permute-start.2 = (bf16[512,1024]{1,0:T(8,128)(2,1)S(1)}, bf16[512,1024]{1,0:T(8,128)(2,1)S(1)}, u32[]{:S(2)}, u32[]{:S(2)}) collective-permute-start(bf16[512,1024]{1,0:T(8,128)(2,1)S(1)} %shard_map.78), channel_id=1, source_target_pairs={{0,4},{4,8},{8,12},{12,16},{16,20},{20,24},{24,28},{28,0},{1,5},{5... | collective-permute-start | bytes 3145736 | tf_op jit(solution)/shard_map/ppermute | solution.py:332
  12.2 3.8 %shard_map.75 = (bf16[512,512]{1,0:T(8,128)(2,1)S(1)}, bf16[4096,512]{1,0:T(8,128)(2,1)S(1)}) custom-call(bf16[512,4096]{1,0:T(8,128)(2,1)S(1)} %get-tuple-element.23.x_hbm.x, bf16[4096,1024]{1,0:T(8,128)(2,1)} %w_hbm.3), custom_call_target="tpu_custom_call" | custom-call | flops 2147483648 | bytes 8912896 | tf_op jit(solution)/shard_map/pallas_call | solution.py:77
  16.0 1.9 %collective-permute-start.1 = (bf16[512,512]{1,0:T(8,128)(2,1)S(1)}, bf16[512,512]{1,0:T(8,128)(2,1)S(1)}, u32[]{:S(2)}, u32[]{:S(2)}) collective-permute-start(bf16[512,512]{1,0:T(8,128)(2,1)S(1)} %get-tuple-element.24), channel_id=1, source_target_pairs={{0,4},{4,8},{8,12},{12,16},{16,20},{20,24},{24,28},{28,0},{1,5},{5... | collective-permute-start | bytes 1572872 | tf_op jit(solution)/shard_map/ppermute | solution.py:332
  17.9 0.0 slice-start
  17.9 0.0 slice-done.2
  17.9 0.0 slice-done.3
  17.9 0.0 copy-done
  17.9 0.0 copy-start.1
  17.9 0.0 slice-start.1
  17.9 10.3 %shard_map.76 = (bf16[512,1024]{1,0:T(8,128)(2,1)S(1)}, bf16[512,1024]{1,0:T(8,128)(2,1)S(1)}, bf16[128,1024]{1,0:T(8,128)(2,1)S(1)}) custom-call(bf16[512,4096]{1,0:T(8,128)(2,1)S(1)} %bitcast.6, bf16[4096,512]{1,0:T(8,128)(2,1)S(1)} %get-tuple-element.25.wk_a, bf16[4096,512]{1,0:T(8,128)(2,1)S(1)} %get-tuple-element.26.wk_b, ...), custom_call_target="tpu_custom_call" | custom-call | flops 9663676416 | bytes 20185088 | tf_op jit(solution)/shard_map/pallas_call | solution.py:144
  28.2 0.0 collective-permute-done.km_a
  28.2 5.1 %collective-permute-done.1.km_b = bf16[512,512]{1,0:T(8,128)(2,1)S(1)} collective-permute-done((bf16[512,512]{1,0:T(8,128)(2,1)S(1)}, bf16[512,512]{1,0:T(8,128)(2,1)S(1)}, u32[]{:S(2)}, u32[]{:S(2)}) %collective-permute-start.1) | collective-permute-done | bytes 524320 | tf_op jit(solution)/shard_map/ppermute | solution.py:332
  33.3 0.0 copy-done.1
  33.3 2.1 %shard_map.85.p = bf16[8,128,1024]{2,1,0:T(8,128)(2,1)S(1)} custom-call(s32[8]{0:T(128)S(1)} %copy-done.1, bf16[128,1024]{1,0:T(8,128)(2,1)S(1)} %get-tuple-element.35.q, bf16[512,512]{1,0:T(8,128)(2,1)S(1)} %collective-permute-done.km_a, bf16[512,512]{1,0:T(8,128)(2,1)S(1)} %collective-permute-done.1.km_b, bf16[512,1024]{1,0:T(8,128)(2,1)S(1)} %get-tuple-element.27.ko), custom_call_target="tpu_custom_call" | custom-call | flops 268435456 | tf_op jit(solution)/shard_map/pallas_call | solution.py:227
  35.4 0.0 collective-permute-done.2.vm
  35.4 0.0 slice-done
  35.4 0.0 slice-done.1
  35.5 1.9 %shard_map.86 = (bf16[128,2304]{1,0:T(8,128)(2,1)S(1)}, bf16[128,1792]{1,0:T(8,128)(2,1)S(1)}) custom-call(bf16[8,128,1024]{2,1,0:T(8,128)(2,1)S(1)} %shard_map.85.p, bf16[512,1024]{1,0:T(8,128)(2,1)S(1)} %collective-permute-done.2.vm, bf16[512,1024]{1,0:T(8,128)(2,1)S(1)} %get-tuple-element.28.vo, bf16[1024,4096]{1,0:T(8,128)(2,1)S(1)} %bitcast.3), custom_call_target="tpu_custom_call" | custom-call | flops 1342177280 | bytes 8388608 | tf_op jit(solution)/shard_map/pallas_call | solution.py:270
  37.3 2.0 %collective-permute-start.6 = (bf16[128,2304]{1,0:T(8,128)(2,1)S(1)}, bf16[128,2304]{1,0:T(8,128)(2,1)S(1)}, u32[]{:S(2)}, u32[]{:S(2)}) collective-permute-start(bf16[128,2304]{1,0:T(8,128)(2,1)S(1)} %get-tuple-element.37), channel_id=1, source_target_pairs={{0,1},{1,0},{2,3},{3,2},{4,5},{5,4},{6,7},{7,6},{8,9},{9,8},{10,11... | collective-permute-start | bytes 1769480 | tf_op jit(solution)/shard_map/ppermute | solution.py:336
  39.4 1.5 %collective-permute-start.4 = (bf16[128,1792]{1,0:T(8,128)(2,1)S(1)}, bf16[128,1792]{1,0:T(8,128)(2,1)S(1)}, u32[]{:S(2)}, u32[]{:S(2)}) collective-permute-start(bf16[128,1792]{1,0:T(8,128)(2,1)S(1)} %get-tuple-element.36), channel_id=1, source_target_pairs={{0,2},{1,3},{2,0},{3,1},{4,6},{5,7},{6,4},{7,5},{8,10},{9,11},{10,... | collective-permute-start | bytes 1376264 | tf_op jit(solution)/shard_map/ppermute | solution.py:336
  40.9 2.8 %shard_map.73.q = bf16[256,1024]{1,0:T(8,128)(2,1)S(1)} custom-call(bf16[512,4096]{1,0:T(8,128)(2,1)S(1)} %bitcast.7, bf16[4096,1024]{1,0:T(8,128)(2,1)S(1)} %bitcast.5), custom_call_target="tpu_custom_call" | custom-call | flops 2147483648 | bytes 11010048 | tf_op jit(solution)/shard_map/pallas_call | solution.py:173
  43.7 2.1 %shard_map.77.p = bf16[8,128,1024]{2,1,0:T(8,128)(2,1)S(1)} custom-call(s32[8]{0:T(128)S(1)} %copy-done.1, bf16[256,1024]{1,0:T(8,128)(2,1)S(1)} %shard_map.73.q, bf16[512,512]{1,0:T(8,128)(2,1)S(1)} %collective-permute-done.km_a, bf16[512,512]{1,0:T(8,128)(2,1)S(1)} %collective-permute-done.1.km_b, bf16[512,1024]{1,0:T(8,128)(2,1)S(1)} %get-tuple-element.27.ko), custom_call_target="tpu_custom_call" | custom-call | flops 268435456 | tf_op jit(solution)/shard_map/pallas_call | solution.py:227
  45.9 1.5 %shard_map.79 = (bf16[128,2304]{1,0:T(8,128)(2,1)S(1)}, bf16[128,1024]{1,0:T(8,128)(2,1)S(1)}) custom-call(bf16[8,128,1024]{2,1,0:T(8,128)(2,1)S(1)} %shard_map.77.p, bf16[512,1024]{1,0:T(8,128)(2,1)S(1)} %collective-permute-done.2.vm, bf16[512,1024]{1,0:T(8,128)(2,1)S(1)} %get-tuple-element.28.vo, bf16[1024,4096]{1,0:T(8,128)(2,1)S(1)} %bitcast.3), custom_call_target="tpu_custom_call" | custom-call | flops 872415232 | bytes 4718592 | tf_op jit(solution)/shard_map/pallas_call | solution.py:297
  47.4 0.6 collective-permute-start.3
  47.9 2.1 %shard_map.80.p = bf16[8,128,1024]{2,1,0:T(8,128)(2,1)S(1)} custom-call(s32[8]{0:T(128)S(1)} %copy-done.1, bf16[256,1024]{1,0:T(8,128)(2,1)S(1)} %shard_map.73.q, bf16[512,512]{1,0:T(8,128)(2,1)S(1)} %collective-permute-done.km_a, bf16[512,512]{1,0:T(8,128)(2,1)S(1)} %collective-permute-done.1.km_b, bf16[512,1024]{1,0:T(8,128)(2,1)S(1)} %get-tuple-element.27.ko), custom_call_target="tpu_custom_call" | custom-call | flops 268435456 | tf_op jit(solution)/shard_map/pallas_call | solution.py:227
  50.1 1.3 %shard_map.81 = (bf16[128,1792]{1,0:T(8,128)(2,1)S(1)}, bf16[128,1024]{1,0:T(8,128)(2,1)S(1)}) custom-call(bf16[8,128,1024]{2,1,0:T(8,128)(2,1)S(1)} %shard_map.80.p, bf16[512,1024]{1,0:T(8,128)(2,1)S(1)} %collective-permute-done.2.vm, bf16[512,1024]{1,0:T(8,128)(2,1)S(1)} %get-tuple-element.28.vo, bf16[1024,4096]{1,0:T(8,128)(2,1)S(1)} %bitcast.3), custom_call_target="tpu_custom_call" | custom-call | flops 738197504 | bytes 3670016 | tf_op jit(solution)/shard_map/pallas_call | solution.py:297
  51.4 2.2 %collective-permute-done.6.got = bf16[128,2304]{1,0:T(8,128)(2,1)S(1)} collective-permute-done((bf16[128,2304]{1,0:T(8,128)(2,1)S(1)}, bf16[128,2304]{1,0:T(8,128)(2,1)S(1)}, u32[]{:S(2)}, u32[]{:S(2)}) %collective-permute-start.6) | collective-permute-done | bytes 589856 | tf_op jit(solution)/shard_map/ppermute | solution.py:336
  53.6 0.8 %shard_map.88 = bf16[128,2304]{1,0:T(8,128)(2,1)S(1)} custom-call(bf16[128,1024]{1,0:T(8,128)(2,1)S(1)} %get-tuple-element.31.ctx, bf16[1024,4096]{1,0:T(8,128)(2,1)S(1)} %bitcast.3, bf16[128,2304]{1,0:T(8,128)(2,1)S(1)} %collective-permute-done.6.got), custom_call_target="tpu_custom_call" | custom-call | flops 603979776 | bytes 5570560 | tf_op jit(solution)/shard_map/pallas_call | solution.py:320
  54.4 2.1 %collective-permute-start.7 = (bf16[128,2304]{1,0:T(8,128)(2,1)S(1)}, bf16[128,2304]{1,0:T(8,128)(2,1)S(1)}, u32[]{:S(2)}, u32[]{:S(2)}) collective-permute-start(bf16[128,2304]{1,0:T(8,128)(2,1)S(1)} %shard_map.88), channel_id=1, source_target_pairs={{0,2},{1,3},{2,0},{3,1},{4,6},{5,7},{6,4},{7,5},{8,10},{9,11},{10,... | collective-permute-start | bytes 1769480 | tf_op jit(solution)/shard_map/ppermute | solution.py:336
  56.5 0.1 collective-permute-start.8
  56.5 0.0 collective-permute-done.4.got
  56.5 0.7 shard_map.87
  57.2 2.0 %collective-permute-start.5 = (bf16[128,1792]{1,0:T(8,128)(2,1)S(1)}, bf16[128,1792]{1,0:T(8,128)(2,1)S(1)}, u32[]{:S(2)}, u32[]{:S(2)}) collective-permute-start(bf16[128,1792]{1,0:T(8,128)(2,1)S(1)} %shard_map.87), channel_id=1, source_target_pairs={{0,1},{1,0},{2,3},{3,2},{4,5},{5,4},{6,7},{7,6},{8,9},{9,8},{10,11... | collective-permute-start | bytes 1376264 | tf_op jit(solution)/shard_map/ppermute | solution.py:336
  59.2 1.5 %shard_map.82.q = bf16[128,1024]{1,0:T(8,128)(2,1)S(1)} custom-call(bf16[512,4096]{1,0:T(8,128)(2,1)S(1)} %bitcast.8, bf16[4096,1024]{1,0:T(8,128)(2,1)S(1)} %bitcast.5), custom_call_target="tpu_custom_call" | custom-call | flops 1073741824 | bytes 9699328 | tf_op jit(solution)/shard_map/pallas_call | solution.py:173
  60.7 2.1 %shard_map.83.p = bf16[8,128,1024]{2,1,0:T(8,128)(2,1)S(1)} custom-call(s32[8]{0:T(128)S(1)} %copy-done.1, bf16[128,1024]{1,0:T(8,128)(2,1)S(1)} %shard_map.82.q, bf16[512,512]{1,0:T(8,128)(2,1)S(1)} %collective-permute-done.km_a, bf16[512,512]{1,0:T(8,128)(2,1)S(1)} %collective-permute-done.1.km_b, bf16[512,1024]{1,0:T(8,128)(2,1)S(1)} %get-tuple-element.27.ko), custom_call_target="tpu_custom_call" | custom-call | flops 268435456 | tf_op jit(solution)/shard_map/pallas_call | solution.py:227
  62.8 1.9 %shard_map.84.own = f32[128,4096]{1,0:T(8,128)S(1)} custom-call(bf16[8,128,1024]{2,1,0:T(8,128)(2,1)S(1)} %shard_map.83.p, bf16[512,1024]{1,0:T(8,128)(2,1)S(1)} %collective-permute-done.2.vm, bf16[512,1024]{1,0:T(8,128)(2,1)S(1)} %get-tuple-element.28.vo, bf16[1024,4096]{1,0:T(8,128)(2,1)S(1)} %bitcast.3), custom_call_target="tpu_custom_call" | custom-call | flops 1342177280 | bytes 8388608 | tf_op jit(solution)/shard_map/pallas_call | solution.py:270
  64.7 9.2 %collective-permute-done.8.yb = bf16[128,1792]{1,0:T(8,128)(2,1)S(1)} collective-permute-done((bf16[128,1792]{1,0:T(8,128)(2,1)S(1)}, bf16[128,1792]{1,0:T(8,128)(2,1)S(1)}, u32[]{:S(2)}, u32[]{:S(2)}) %collective-permute-start.8) | collective-permute-done | bytes 458784 | tf_op jit(solution)/shard_map/ppermute | solution.py:336
  73.9 0.0 collective-permute-done.3.xa
  73.9 0.0 collective-permute-done.5.xb
  73.9 0.0 collective-permute-done.7.ya
  73.9 1.1 %shard_map.89 = bf16[1,128,4096]{2,1,0:T(8,128)(2,1)} custom-call(f32[128,4096]{1,0:T(8,128)S(1)} %shard_map.84.own, bf16[128,2304]{1,0:T(8,128)(2,1)S(1)} %collective-permute-done.3.xa, bf16[128,1792]{1,0:T(8,128)(2,1)S(1)} %collective-permute-done.5.xb, bf16[128,2304]{1,0:T(8,128)(2,1)S(1)} %collective-permute-done.7.ya, ...), custom_call_target="tpu_custom_call" | custom-call | flops 1572864 | bytes 7340032 | tf_op jit(solution)/shard_map/pallas_call | solution.py:358
  (2 shorter events, 0.0 us)
Async XLA Ops:
  0.0 5.9 %copy-start.2 = (bf16[4096,1024]{1,0:T(8,128)(2,1)S(1)}, bf16[4096,1024]{1,0:T(8,128)(2,1)}, u32[]{:S(2)}) copy-start(bf16[4096,1024]{1,0:T(8,128)(2,1)} %refs_0_.1) | copy-start | bytes 25165828
  0.0 17.9 %slice-start.2 = ((s8[8388608]{0:T(1024)(128)(4,1)}), s8[4194304]{0:T(1024)(128)(4,1)S(1)}, s32[]{:S(2)}) async-start(s8[8388608]{0:T(1024)(128)(4,1)} %bitcast.4), calls=%async_computation.2 | async-start | bytes 8388608
  4.2 24.0 %collective-permute-start = (bf16[512,512]{1,0:T(8,128)(2,1)S(1)}, bf16[512,512]{1,0:T(8,128)(2,1)S(1)}, u32[]{:S(2)}, u32[]{:S(2)}) collective-permute-start(bf16[512,512]{1,0:T(8,128)(2,1)S(1)} %get-tuple-element.22), channel_id=1, source_target_pairs={{0,4},{4,8},{8,12},{12,16},{16,20},{20,24},{24,28},{28,0},{1,5},{5... | collective-permute-start | bytes 1572872 | tf_op jit(solution)/shard_map/ppermute | solution.py:332
  5.9 12.0 %slice-start.3 = ((s8[8388608]{0:T(1024)(128)(4,1)}), s8[4194304]{0:T(1024)(128)(4,1)S(1)}, s32[]{:S(2)}) async-start(s8[8388608]{0:T(1024)(128)(4,1)} %bitcast.4), calls=%async_computation.3 | async-start | bytes 8388608
  10.6 7.3 %copy-start = (bf16[1,512,4096]{2,1,0:T(8,128)(2,1)S(1)}, bf16[1,512,4096]{2,1,0:T(8,128)(2,1)}, u32[]{:S(2)}) copy-start(bf16[1,512,4096]{2,1,0:T(8,128)(2,1)} %param.7) | copy-start | bytes 12582916
  10.6 24.8 %collective-permute-start.2 = (bf16[512,1024]{1,0:T(8,128)(2,1)S(1)}, bf16[512,1024]{1,0:T(8,128)(2,1)S(1)}, u32[]{:S(2)}, u32[]{:S(2)}) collective-permute-start(bf16[512,1024]{1,0:T(8,128)(2,1)S(1)} %shard_map.78), channel_id=1, source_target_pairs={{0,4},{4,8},{8,12},{12,16},{16,20},{20,24},{24,28},{28,0},{1,5},{5... | collective-permute-start | bytes 3145736 | tf_op jit(solution)/shard_map/ppermute | solution.py:332
  16.0 17.3 %collective-permute-start.1 = (bf16[512,512]{1,0:T(8,128)(2,1)S(1)}, bf16[512,512]{1,0:T(8,128)(2,1)S(1)}, u32[]{:S(2)}, u32[]{:S(2)}) collective-permute-start(bf16[512,512]{1,0:T(8,128)(2,1)S(1)} %get-tuple-element.24), channel_id=1, source_target_pairs={{0,4},{4,8},{8,12},{12,16},{16,20},{20,24},{24,28},{28,0},{1,5},{5... | collective-permute-start | bytes 1572872 | tf_op jit(solution)/shard_map/ppermute | solution.py:332
  17.9 17.6 %slice-start = ((s8[8388608]{0:T(1024)(128)(4,1)}), s8[4194304]{0:T(1024)(128)(4,1)S(1)}, s32[]{:S(2)}) async-start(s8[8388608]{0:T(1024)(128)(4,1)} %bitcast.2), calls=%async_computation | async-start | bytes 8388608
  17.9 15.4 %copy-start.1 = (s32[8]{0:T(128)S(1)}, s32[8]{0:T(128)}, u32[]{:S(2)}) copy-start(s32[8]{0:T(128)} %lens.7) | copy-start | bytes 100
  17.9 17.5 %slice-start.1 = ((s8[8388608]{0:T(1024)(128)(4,1)}), s8[4194304]{0:T(1024)(128)(4,1)S(1)}, s32[]{:S(2)}) async-start(s8[8388608]{0:T(1024)(128)(4,1)} %bitcast.2), calls=%async_computation.1 | async-start | bytes 8388608
  37.3 16.3 %collective-permute-start.6 = (bf16[128,2304]{1,0:T(8,128)(2,1)S(1)}, bf16[128,2304]{1,0:T(8,128)(2,1)S(1)}, u32[]{:S(2)}, u32[]{:S(2)}) collective-permute-start(bf16[128,2304]{1,0:T(8,128)(2,1)S(1)} %get-tuple-element.37), channel_id=1, source_target_pairs={{0,1},{1,0},{2,3},{3,2},{4,5},{5,4},{6,7},{7,6},{8,9},{9,8},{10,11... | collective-permute-start | bytes 1769480 | tf_op jit(solution)/shard_map/ppermute | solution.py:336
  39.4 17.2 %collective-permute-start.4 = (bf16[128,1792]{1,0:T(8,128)(2,1)S(1)}, bf16[128,1792]{1,0:T(8,128)(2,1)S(1)}, u32[]{:S(2)}, u32[]{:S(2)}) collective-permute-start(bf16[128,1792]{1,0:T(8,128)(2,1)S(1)} %get-tuple-element.36), channel_id=1, source_target_pairs={{0,2},{1,3},{2,0},{3,1},{4,6},{5,7},{6,4},{7,5},{8,10},{9,11},{10,... | collective-permute-start | bytes 1376264 | tf_op jit(solution)/shard_map/ppermute | solution.py:336
  47.4 26.6 %collective-permute-start.3 = (bf16[128,2304]{1,0:T(8,128)(2,1)S(1)}, bf16[128,2304]{1,0:T(8,128)(2,1)S(1)}, u32[]{:S(2)}, u32[]{:S(2)}) collective-permute-start(bf16[128,2304]{1,0:T(8,128)(2,1)S(1)} %get-tuple-element.33), channel_id=1, source_target_pairs={{0,1},{1,0},{2,3},{3,2},{4,5},{5,4},{6,7},{7,6},{8,9},{9,8},{10,11... | collective-permute-start | bytes 1769480 | tf_op jit(solution)/shard_map/ppermute | solution.py:336
  54.4 19.5 %collective-permute-start.7 = (bf16[128,2304]{1,0:T(8,128)(2,1)S(1)}, bf16[128,2304]{1,0:T(8,128)(2,1)S(1)}, u32[]{:S(2)}, u32[]{:S(2)}) collective-permute-start(bf16[128,2304]{1,0:T(8,128)(2,1)S(1)} %shard_map.88), channel_id=1, source_target_pairs={{0,2},{1,3},{2,0},{3,1},{4,6},{5,7},{6,4},{7,5},{8,10},{9,11},{10,... | collective-permute-start | bytes 1769480 | tf_op jit(solution)/shard_map/ppermute | solution.py:336
  56.5 17.5 %collective-permute-start.8 = (bf16[128,1792]{1,0:T(8,128)(2,1)S(1)}, bf16[128,1792]{1,0:T(8,128)(2,1)S(1)}, u32[]{:S(2)}, u32[]{:S(2)}) collective-permute-start(bf16[128,1792]{1,0:T(8,128)(2,1)S(1)} %get-tuple-element.38), channel_id=1, source_target_pairs={{0,2},{1,3},{2,0},{3,1},{4,6},{5,7},{6,4},{7,5},{8,10},{9,11},{10,... | collective-permute-start | bytes 1376264 | tf_op jit(solution)/shard_map/ppermute | solution.py:336
  57.2 16.7 %collective-permute-start.5 = (bf16[128,1792]{1,0:T(8,128)(2,1)S(1)}, bf16[128,1792]{1,0:T(8,128)(2,1)S(1)}, u32[]{:S(2)}, u32[]{:S(2)}) collective-permute-start(bf16[128,1792]{1,0:T(8,128)(2,1)S(1)} %shard_map.87), channel_id=1, source_target_pairs={{0,1},{1,0},{2,3},{3,2},{4,5},{5,4},{6,7},{7,6},{8,9},{9,8},{10,11... | collective-permute-start | bytes 1376264 | tf_op jit(solution)/shard_map/ppermute | solution.py:336
